TPU v7x, 32 devices: a whole 2x2x4 slice. The times are simulated.
32 devices in a mesh: wide: 8 (over y, x, core), narrow: 4 (over z).
Axes of the slice: x: 2, y: 2, z: 4, core: 2. Of those that a mesh axis runs over, the one named last changes fastest.
Arguments:
- tokens: bfloat16 [2048, 2048], P('wide', 'narrow'), may hold values from -6 to 6
- gain_attn: bfloat16 [2048], P('narrow'), may hold values from 0.5 to 1.5
- w_query: bfloat16 [2048, 2048], P('wide', 'narrow'), may hold values from -0.1875 to 0.1875
- w_key: bfloat16 [2048, 2048], P('wide', 'narrow'), may hold values from -0.1875 to 0.1875
- w_value: bfloat16 [2048, 2048], P('wide', 'narrow'), may hold values from -0.125 to 0.125
- w_out: bfloat16 [2048, 2048], P('wide', 'narrow'), may hold values from -0.5 to 0.5
- gain_ffn: bfloat16 [2048], P('narrow'), may hold values from 0.5 to 1.5
- w_router: bfloat16 [2048, 4], P('wide'), may hold values from -0.09375 to 0.09375
- w_gate: bfloat16 [2048, 4, 5632], P('wide', None, 'narrow'), may hold values from -0.125 to 0.125
- w_up: bfloat16 [2048, 4, 5632], P('wide', None, 'narrow'), may hold values from -0.125 to 0.125
- w_down: bfloat16 [2048, 4, 5632], P('wide', None, 'narrow'), may hold values from -0.109375 to 0.109375
- segment: int32 [8, 256], P('wide'), may hold values from 0 to 12, never falling along the last dimension, each value on 1 to 102 neighbouring positions
- parents: int32 [8, 13], P('wide'), may hold values from 0 to 4, as said below
- expert_ids: int32 [2048, 2], P('wide'), may hold values from 0 to 3, all different within a row
- slot_order: int32 [8, 256], P('wide'), may hold values from 0 to 255, each once within a row
- cotangent: bfloat16 [2048, 2048], P('wide', 'narrow'), may hold values from -6 to 6
Outputs:
- output: bfloat16 [2048, 2048], P('wide', 'narrow')
- grad_tokens: float32 [2048, 2048], P('wide', 'narrow')
- grad_gain_attn: float32 [2048], P('narrow')
- grad_w_query: float32 [2048, 2048], P('wide', 'narrow')
- grad_w_key: float32 [2048, 2048], P('wide', 'narrow')
- grad_w_value: float32 [2048, 2048], P('wide', 'narrow')
- grad_w_out: float32 [2048, 2048], P('wide', 'narrow')
- grad_gain_ffn: float32 [2048], P('narrow')
- grad_w_router: float32 [2048, 4], P('wide')
- grad_w_gate: float32 [2048, 4, 5632], P('wide', None, 'narrow')
- grad_w_up: float32 [2048, 4, 5632], P('wide', None, 'narrow')
- grad_w_down: float32 [2048, 4, 5632], P('wide', None, 'narrow')
Inputs may be any that keep to these rules, and one draw needn't show every extreme that they name: In every tree, segment 0 is the trunk and has entry 0; segments 1 to 4 have parent 0; segments 5 to 12 have parents among 1 to 4, two on each. `segment`: segment numbers never fall within a tree; all 13 segments are present. `expert_ids`: the two experts of a token differ. `slot_order`: each row is a permutation of the numbers below 256.
All inputs are finite; a program needn't handle non-finite values.
Results may differ from a plain program's by a relative error of at most 0.03.
Values may be sent and summed in bfloat16 or wider, within the bound.
A program may use at most 448 MiB of HBM per device.

v0:
```python
import math

import jax
import jax.numpy as jnp
from jax import lax
from jax.experimental import pallas as pl
from jax.experimental.pallas import tpu as pltpu
from jax.sharding import PartitionSpec as P

HEAD_DIM = 128
EXPERTS = 4
SEGS = 13
CAP = 144
SLOTS = EXPERTS * CAP
NORM_EPS = 1e-05
NEG_FILL = -1e30
ROPE_BASE = 10000.0
BF = jnp.bfloat16
F32 = jnp.float32


def mm(left, right, dims):
    return lax.dot_general(left, right, (dims, ((), ())), preferred_element_type=F32)


def rows_cols(left, right):
    return mm(left, right, ((1,), (0,)))


def rows_rows(left, right):
    return mm(left, right, ((1,), (1,)))


def cols_cols(left, right):
    return mm(left, right, ((0,), (0,)))


def tree_layout(segment_row, parent_row):
    seg_ids = jnp.arange(SEGS, dtype=jnp.int32)
    member = segment_row[:, None] == seg_ids[None, :]
    parent_of = (parent_row[:, None] == seg_ids[None, :]) & (seg_ids[:, None] != 0)
    itself = seg_ids[:, None] == seg_ids[None, :]
    reach = itself
    for _ in range(3):
        reach = itself | jnp.any(parent_of[:, :, None] & reach[None, :, :], axis=1)
    counts = member.astype(jnp.int32)
    lengths = jnp.sum(counts, 0)
    starts = jnp.sum(jnp.where(seg_ids[None, :] < seg_ids[:, None], lengths[None, :], 0), 1)
    before = jnp.sum(jnp.where(reach, lengths[None, :], 0), 1) - lengths
    row_at = jnp.arange(segment_row.shape[0], dtype=jnp.int32)
    places = jnp.sum(counts * (before - starts)[None, :], 1) + row_at
    member_low = member.astype(BF)
    lineage = rows_cols(member_low, reach.astype(BF)).astype(BF)
    shared = rows_rows(lineage, member_low) > 0.5
    seen = shared & (row_at[None, :] <= row_at[:, None])
    return seen, places.astype(F32)


def route(expert_row, slot_rank):
    expert_range = jnp.arange(EXPERTS, dtype=jnp.int32)
    hot_first = (expert_row[:, 0:1] == expert_range[None, :]).astype(F32)
    hot_second = (expert_row[:, 1:2] == expert_range[None, :]).astype(F32)
    earlier = (slot_rank[None, :] < slot_rank[:, None]).astype(BF)
    count_first = rows_cols(earlier, hot_first.astype(BF))
    count_second = rows_cols(earlier, hot_second.astype(BF))
    ahead_first = jnp.sum(count_first * hot_first, 1)
    ahead_second = jnp.sum((count_second + jnp.sum(hot_first, 0)[None, :]) * hot_second, 1)
    slot_index = jnp.stack([ahead_first, ahead_second], 1).astype(jnp.int32)
    kept = slot_index < CAP
    flat_slot = jnp.where(kept, expert_row * CAP + slot_index, SLOTS)
    slot_range = jnp.arange(SLOTS, dtype=jnp.int32)
    pick_first = flat_slot[:, 0:1] == slot_range[None, :]
    pick_second = flat_slot[:, 1:2] == slot_range[None, :]
    return hot_first, hot_second, kept.astype(F32), pick_first, pick_second


def rotate(vectors, cosines, sines):
    half_dim = HEAD_DIM // 2
    first_half = vectors[..., :half_dim]
    second_half = vectors[..., half_dim:]
    return jnp.concatenate(
        [
            first_half * cosines - second_half * sines,
            second_half * cosines + first_half * sines,
        ],
        -1,
    )


def gate_pair(logits, hot_first, hot_second):
    chances = jax.nn.softmax(logits, axis=-1)
    first_share = jnp.sum(chances * hot_first, 1)
    second_share = jnp.sum(chances * hot_second, 1)
    pair_total = first_share + second_share
    return (first_share / pair_total, second_share / pair_total)


def two_parts(column):
    high = column.astype(BF)
    return high, (column - high.astype(F32)).astype(BF)


MESH = pl.DeviceIdType.MESH
NEAR = 3


def low_dot(left, right):
    return jnp.dot(left, right, preferred_element_type=F32)


def places_of(n):
    return [lax.rem(n + step, 4) for step in (1, 2, 3)], [lax.rem(n + 4 - step, 4) for step in (1, 2, 3)]


def plane_of(chip):
    x, y = lax.rem(chip, 2), chip // 2
    return [2 * y + 1 - x, 2 * (1 - y) + x, 2 * (1 - y) + 1 - x]


def greet(narrow_peers, plane_peers, chip, core, mate):
    barrier = pltpu.get_barrier_semaphore()
    count = 0
    for peer in narrow_peers:
        pl.semaphore_signal(barrier, inc=1, device_id={"narrow": peer}, device_id_type=MESH)
        count += 1
    for peer in plane_peers:
        pl.semaphore_signal(
            barrier, inc=1, device_id={"wide": 2 * peer + core}, device_id_type=MESH
        )
        count += 1
    if mate:
        pl.semaphore_signal(
            barrier, inc=1, device_id={"wide": 2 * chip + 1 - core}, device_id_type=MESH
        )
        count += 1
    pl.semaphore_wait(barrier, count)


class Links:
    def __init__(self, sent, landed, local):
        self.sent, self.landed, self.local = sent, landed, local
        self.used, self.local_used = 0, 0
        self.waits = []

    def slot(self):
        self.used += 1
        return self.used - 1

    def send(self, source, target, device, slot, when=None):
        copy = pltpu.make_async_remote_copy(
            src_ref=source,
            dst_ref=target,
            send_sem=self.sent.at[slot],
            recv_sem=self.landed.at[slot],
            device_id=device,
            device_id_type=MESH,
        )
        if when is None:
            copy.start()
        else:
            pl.when(when)(copy.start)
        self.waits.append((copy, when))

    def land(self, target, device, slot, when=None):
        copy = pltpu.make_async_remote_copy(
            src_ref=target,
            dst_ref=target,
            send_sem=self.sent.at[slot],
            recv_sem=self.landed.at[slot],
            device_id=device,
            device_id_type=MESH,
        )
        if when is None:
            copy.wait_recv()
        else:
            pl.when(when)(copy.wait_recv)

    def move(self, source, target):
        copy = pltpu.make_async_copy(source, target, self.local.at[self.local_used])
        self.local_used += 1
        copy.start()
        self.waits.append((copy, "local"))
        return copy

    def finish(self):
        for copy, when in self.waits:
            if when == "local":
                copy.wait()
            elif when is None:
                copy.wait_send()
            else:
                pl.when(when)(copy.wait_send)


class Chain:
    def __init__(self, links, n, block):
        self.links, self.n, self.block = links, n, block
        self.slots = [(links.slot(), links.slot()) for _ in range(3)]

    def start(self, step):
        n, links = self.n, self.links
        right, left = self.slots[step]
        block = self.block(lax.rem(n + 4 - step, 4))
        links.send(
            block, block, {"narrow": lax.rem(n + 1, 4)}, right,
            (n < 3) & (n >= step),
        )
        block = self.block(lax.rem(n + step, 4))
        links.send(
            block, block, {"narrow": lax.rem(n + 3, 4)}, left,
            (n > 0) & (n + step <= 3),
        )

    def land(self, step):
        n, links = self.n, self.links
        right, left = self.slots[step]
        links.land(
            self.block(lax.rem(n + 7 - step, 4)), {"narrow": lax.rem(n + 3, 4)}, right,
            n >= step + 1,
        )
        links.land(
            self.block(lax.rem(n + 1 + step, 4)), {"narrow": lax.rem(n + 1, 4)}, left,
            n + 1 + step <= 3,
        )


class LineSum:
    def __init__(self, links, n, outbox, inbox):
        self.links, self.n, self.outbox, self.inbox = links, n, outbox, inbox
        self.inner = (n == 1) | (n == 2)
        self.outer = (n == 0) | (n == 3)
        self.targets = [self.owner(step) for step in range(NEAR)]
        self.next = 1 + lax.rem(n, 2)
        self.slots = [links.slot() for _ in range(6)]

    def owner(self, step):
        return lax.rem((4 - step) * self.n + (3 - step), 5)

    def put(self, step, part):
        self.outbox[step] = part.astype(BF)
        self.set_out(step)

    def set_out(self, step):
        links, outbox, inbox = self.links, self.outbox, self.inbox
        goal = {"narrow": self.next if step == 0 else self.targets[step]}
        far, near = self.slots[2 * step], self.slots[2 * step + 1]
        if step == 0:
            links.send(outbox.at[0], inbox.at[3], goal, far, self.outer)
            links.send(outbox.at[0], inbox.at[0], goal, near, self.inner)
        elif step == 1:
            links.send(outbox.at[1], inbox.at[1], goal, far, self.outer)
            links.send(outbox.at[1], inbox.at[0], goal, near, self.inner)
        else:
            links.send(outbox.at[2], inbox.at[2], goal, far, self.outer)

    def join(self):
        links, outbox, inbox = self.links, self.outbox, self.inbox
        home = {"narrow": 3 * (self.n // 2)}
        links.land(inbox.at[3], home, self.slots[0], self.inner)

        @pl.when(self.inner)
        def _():
            outbox[2] = (outbox[2].astype(F32) + inbox[3].astype(F32)).astype(BF)

    def relay(self):
        self.join()
        goal = {"narrow": self.targets[2]}
        self.links.send(
            self.outbox.at[2], self.inbox.at[1], goal, self.slots[5], self.inner
        )

    def early(self, own):
        links, inbox = self.links, self.inbox
        other = {"narrow": lax.rem(self.n + 1, 4)}
        links.land(inbox.at[0], other, self.slots[1], self.inner)
        links.land(inbox.at[0], other, self.slots[3], self.outer)
        links.land(inbox.at[1], other, self.slots[2], self.inner)

        @pl.when(self.outer)
        def _():
            inbox[1] = jnp.zeros(inbox.shape[1:], BF)

        return own + inbox[0].astype(F32) + inbox[1].astype(F32)

    def total(self, own):
        links, inbox = self.links, self.inbox
        outer, inner = self.outer, self.inner
        other = {"narrow": lax.rem(self.n + 1, 4)}
        links.land(inbox.at[0], other, self.slots[1], inner)
        links.land(inbox.at[0], other, self.slots[3], outer)
        links.land(inbox.at[1], other, self.slots[2], inner)
        links.land(inbox.at[1], other, self.slots[5], outer)
        links.land(inbox.at[2], other, self.slots[4], inner)

        @pl.when(outer)
        def _():
            inbox[2] = jnp.zeros(inbox.shape[1:], BF)

        for index in range(3):
            own = own + inbox[index].astype(F32)
        return own


class PlaneGather:
    def __init__(self, links, chip, core, plane, mate, source, blocks):
        self.links, self.chip, self.core, self.plane, self.mate = links, chip, core, plane, mate
        self.blocks = blocks
        self.slots = [links.slot() for _ in range(4)]
        self.mate_slots = [links.slot() for _ in range(4)]
        own = 2 * chip + core
        for side in range(2):
            links.send(source, blocks.at[own], self.at_plane(plane[side]), self.slots[side])
        links.send(source, blocks.at[own], mate, self.mate_slots[3])

    def at_plane(self, peer):
        return {"wide": 2 * peer + self.core}

    def half(self, peer, side):
        rows = self.blocks.shape[1] // 2
        return self.blocks.at[2 * peer + self.core, pl.ds(side * rows, rows), :]

    def pass_on(self):
        links, plane = self.links, self.plane
        for side in range(2):
            block = self.blocks.at[2 * plane[side] + self.core]
            links.land(block, self.at_plane(plane[side]), self.slots[side])
            part = self.half(plane[side], side)
            links.send(part, part, self.at_plane(plane[1 - side]), self.slots[2 + side])
            links.send(block, block, self.mate, self.mate_slots[side])

    def far(self):
        links, plane = self.links, self.plane
        for side in range(2):
            links.land(
                self.half(plane[2], side), self.at_plane(plane[1 - side]), self.slots[2 + side]
            )
        block = self.blocks.at[2 * plane[2] + self.core]
        links.send(block, block, self.mate, self.mate_slots[2])

    def finish(self):
        links, plane = self.links, self.plane
        for step in range(NEAR):
            block = self.blocks.at[2 * plane[step] + 1 - self.core]
            links.land(block, self.mate, self.mate_slots[step])
        links.land(self.blocks.at[2 * self.chip + 1 - self.core], self.mate, self.mate_slots[3])


FRONT_SLOTS = 104


def front_body(
    tok_ref, cot_ref, gains_ref, wq_ref, wk_ref, wv_ref, wo_ref, router_ref, gate_ref, up_ref,
    down_ref, segment_ref, parents_ref, ids_ref, rank_ref,
    qkvw_out, outw_out, expert_out, x_out, dy_out, gate_out, middle_out, hidden_out,
    tokens_out, qkv_out, prob_out, att_out, stat_out, rope_out, pick_out, cols_out,
    raw_proj, seen_at, raw, moved_ref, pack, tok_pack, qkvw, outw, cot_send, y_send, br_send, br_recv, stat_send, stat_recv,
    gate_send, sent, landed, local,
):
    n = lax.axis_index("narrow")
    w = lax.axis_index("wide")
    chip, core = w // 2, lax.rem(w, 2)
    to_z, from_z = places_of(n)
    plane = plane_of(chip)
    links = Links(sent, landed, local)
    mate = {"wide": 2 * chip + 1 - core}

    def at_plane(peer):
        return {"wide": 2 * peer + core}

    token_count, part_width = tok_ref.shape
    rows_each = raw.shape[1]
    raw_loads = [
        links.move(source, raw.at[kind_at]) for kind_at, source in enumerate((gate_ref, up_ref, down_ref))
    ]
    links.waits = []
    greet(to_z, plane, chip, core, True)

    def by_expert(kind_at):
        raw_loads[kind_at].wait()

        def some_rows(index, value):
            rows = pl.ds(pl.multiple_of(index * 32, 32), 32)
            for expert in range(EXPERTS):
                moved_ref[kind_at, expert, rows, :] = raw[kind_at, rows, expert, :]
            return value

        lax.fori_loop(0, rows_each // 32, some_rows, 0)

    tok_pack[0:token_count, :] = tok_ref[...]
    tok_pack[token_count : token_count + 2, :] = gains_ref[...]
    tokens_out[n] = tok_pack[...]
    tok_chain = Chain(links, n, lambda m: tokens_out.at[m])
    tok_chain.start(0)
    wide_shape = (token_count, token_count)
    row_at = lax.broadcasted_iota(jnp.int32, wide_shape, 0)
    col_at = lax.broadcasted_iota(jnp.int32, wide_shape, 1)
    seg_row, rank_row = segment_ref[...], rank_ref[...]
    first_row, second_row = ids_ref[0:1, :], ids_ref[1:2, :]
    stacked = [item.astype(F32) for item in (seg_row, rank_row, first_row, second_row)]
    columns = jnp.concatenate(stacked + [jnp.zeros((124, token_count), F32)], 0).T
    cols_out[...] = columns
    columns = columns.astype(jnp.int32)
    seg_col, rank_col = columns[:, 0:1], columns[:, 1:2]
    segs = parents_ref.shape[1]
    of_seg = lax.broadcasted_iota(jnp.int32, (token_count, segs), 1) == seg_col
    par_col = jnp.sum(
        jnp.where(of_seg, parents_ref[...].astype(F32), 0.0), 1, keepdims=True
    ).astype(jnp.int32)
    seen = ((seg_row == seg_col) | (seg_row == par_col) | (seg_row == 0)) & (col_at <= row_at)
    spots = jnp.sum(jnp.where(seen, 1.0, 0.0), 1, keepdims=True) - 1.0
    lane_at = lax.broadcasted_iota(jnp.int32, (token_count, HEAD_DIM), 1)
    turn = lax.rem(lane_at, HEAD_DIM // 2).astype(F32) * (-2.0 / HEAD_DIM * math.log(ROPE_BASE))
    angles = spots * jnp.exp(turn)
    cosines = jnp.cos(angles)
    sines = jnp.sin(angles) * jnp.where(lane_at < HEAD_DIM // 2, -1.0, 1.0)
    rope_out[0] = cosines
    rope_out[1] = sines
    kind = lax.broadcasted_iota(jnp.int32, (8, token_count), 0)
    hot_first = jnp.where(kind == first_row, 1.0, 0.0)
    hot_second = jnp.where(kind == second_row, 1.0, 0.0)
    earlier = jnp.where(rank_col < rank_row, 1.0, 0.0).astype(BF)
    count_first = low_dot(hot_first.astype(BF), earlier)
    count_second = low_dot(hot_second.astype(BF), earlier)
    count_second = count_second + jnp.sum(hot_first, 1, keepdims=True)
    slot_first = jnp.sum(count_first * hot_first, 0, keepdims=True)
    slot_second = jnp.sum(count_second * hot_second, 0, keepdims=True)
    kept_first = jnp.where(slot_first < CAP, 1.0, 0.0)
    kept_second = jnp.where(slot_second < CAP, 1.0, 0.0)
    flat_first = jnp.where(slot_first < CAP, first_row * CAP + slot_first.astype(jnp.int32), SLOTS)
    flat_second = jnp.where(
        slot_second < CAP, second_row * CAP + slot_second.astype(jnp.int32), SLOTS
    )
    slot_at = lax.broadcasted_iota(jnp.int32, (SLOTS, token_count), 0)
    pick_first = jnp.where(slot_at == flat_first, 1.0, 0.0)
    pick_second = jnp.where(slot_at == flat_second, 1.0, 0.0)
    pick_out[0] = pick_first.astype(BF)
    pick_out[1] = pick_second.astype(BF)
    pick_both = (pick_first + pick_second).astype(BF)

    def column_block(array):
        return lambda m: array.at[:, pl.ds(pl.multiple_of(m * part_width, part_width), part_width)]

    def slot_block(array, owner):
        return array.at[
            pl.ds(pl.multiple_of(owner * CAP, 16), CAP),
            pl.ds(pl.multiple_of(n * part_width, part_width), part_width),
        ]

    def dispatch(rows, buffer, array):
        slots = [links.slot() for _ in range(NEAR)]
        buffer[...] = low_dot(pick_both, rows).astype(BF)
        for step in range(NEAR):
            links.send(
                buffer.at[pl.ds(pl.multiple_of(plane[step] * CAP, 16), CAP), :],
                slot_block(array, chip), at_plane(plane[step]), slots[step],
            )
        own = links.move(
            buffer.at[pl.ds(pl.multiple_of(chip * CAP, 16), CAP), :], slot_block(array, chip)
        )
        return slots, own

    def arrive(array, state):
        slots, own = state
        for step in range(NEAR):
            links.land(slot_block(array, plane[step]), at_plane(plane[step]), slots[step])
        own.wait()
        links.waits = [item for item in links.waits if item[0] is not own]

    dy_state = dispatch(cot_ref[...], cot_send, dy_out)
    dy_chain = Chain(links, n, column_block(dy_out))

    pack[:, 0:512] = wq_ref[...]
    pack[:, 512:1024] = wk_ref[...]
    pack[:, 1024:1536] = wv_ref[...]
    router_rows = jnp.concatenate(
        [router_ref[...].astype(F32), jnp.zeros((128 - EXPERTS, rows_each), F32)], 0
    )
    pack[:, 1536:1664] = router_rows.T.astype(BF)
    in_gather = PlaneGather(links, chip, core, plane, mate, pack, qkvw)
    qkvw[w] = pack[...]
    outw[w] = wo_ref[...]

    tok_chain.land(0)
    tok_chain.start(1)
    by_expert(0)
    tok_chain.land(1)
    tok_chain.start(2)
    arrive(dy_out, dy_state)
    dy_chain.start(0)
    tok_chain.land(2)
    in_gather.pass_on()
    out_gather = PlaneGather(links, chip, core, plane, mate, wo_ref, outw)
    total = jnp.zeros((token_count, 1), F32)
    for m in range(4):
        part = tokens_out[m, 0:token_count, :].astype(F32)
        total = total + jnp.sum(part * part, 1, keepdims=True)
    scale_first = lax.rsqrt(total * (1.0 / (4 * part_width)) + NORM_EPS)
    for m in range(4):
        part = tokens_out[m, 0:token_count, :].astype(F32)
        gain = tokens_out[m, token_count : token_count + 1, :].astype(F32)
        hidden_out[:, m * part_width : (m + 1) * part_width] = (part * scale_first * gain).astype(BF)

    by_expert(1)

    in_gather.far()
    out_gather.pass_on()
    in_gather.finish()
    saved_in = links.move(qkvw, qkvw_out)

    expert_slots = [[links.slot() for _ in range(NEAR)] for _ in range(3)]
    expert_mate = [[links.slot() for _ in range(4)] for _ in range(3)]
    def set_out(kind_at):
        for step in range(NEAR):
            links.send(
                moved_ref.at[kind_at, plane[step]], expert_out.at[kind_at, chip, core],
                at_plane(plane[step]), expert_slots[kind_at][step],
            )
        links.send(
            moved_ref.at[kind_at, chip], expert_out.at[kind_at, chip, core], mate,
            expert_mate[kind_at][3],
        )
        links.move(moved_ref.at[kind_at, chip], expert_out.at[kind_at, chip, core])

    set_out(0)
    set_out(1)

    def pass_on(kind_at):
        for step in range(NEAR):
            block = expert_out.at[kind_at, plane[step], core]
            links.land(block, at_plane(plane[step]), expert_slots[kind_at][step])
            links.send(block, block, mate, expert_mate[kind_at][step])

    def all_there(kind_at):
        for step in range(NEAR):
            links.land(
                expert_out.at[kind_at, plane[step], 1 - core], mate, expert_mate[kind_at][step]
            )
        links.land(expert_out.at[kind_at, chip, 1 - core], mate, expert_mate[kind_at][3])

    dy_chain.land(0)
    dy_chain.start(1)
    by_expert(2)

    score_scale = HEAD_DIM ** (-0.5)

    def one_projection(part, value):
        cols = pl.ds(pl.multiple_of(part * part_width, part_width), part_width)
        weight = qkvw[:, :, cols].reshape(4 * part_width, part_width)
        raw_proj[part] = low_dot(hidden_out[...], weight)
        return value

    lax.fori_loop(0, 3, one_projection, 0)
    seen_at[...] = jnp.where(seen, 1.0, 0.0)

    def one_head(head, value):
        cols = pl.ds(pl.multiple_of(head * HEAD_DIM, HEAD_DIM), HEAD_DIM)
        turned = []
        for part in range(2):
            proj = raw_proj[part, :, cols]
            turned.append(
                (proj * rope_out[0] + pltpu.roll(proj, HEAD_DIM // 2, 1) * rope_out[1]).astype(BF)
            )
            qkv_out[part, :, cols] = turned[part]
        values = raw_proj[2, :, cols].astype(BF)
        qkv_out[2, :, cols] = values
        scores = rows_rows(turned[0], turned[1]) * score_scale
        scores = jnp.where(seen_at[...] > 0.5, scores, NEG_FILL)
        exps = jnp.exp(scores - jnp.max(scores, 1, keepdims=True))
        weights = exps / jnp.sum(exps, 1, keepdims=True)
        prob_out[head] = weights
        att_out[:, cols] = low_dot(weights.astype(BF), values).astype(BF)
        return value

    lax.fori_loop(0, part_width // HEAD_DIM, one_head, 0)

    dy_chain.land(1)
    dy_chain.start(2)
    out_gather.far()

    out_gather.finish()
    links.move(outw, outw_out)

    attended = att_out[...]

    def branch(m):
        weight = outw[pl.ds(2 * m, 2)].reshape(part_width, part_width)
        return rows_rows(attended, weight)

    branch_sum = LineSum(links, n, br_send, br_recv)
    for step in range(NEAR):
        branch_sum.put(step, branch(branch_sum.targets[step]))
    middle = tok_ref[...].astype(F32) + branch(n)
    branch_sum.relay()
    middle = branch_sum.total(middle)
    middle_out[...] = middle
    x_state = dispatch(middle.astype(BF), y_send, x_out)

    def cap_block(owner):
        return lambda m: x_out.at[
            pl.ds(pl.multiple_of(owner * CAP, 16), CAP),
            pl.ds(pl.multiple_of(m * part_width, part_width), part_width),
        ]

    x_chains = [Chain(links, n, cap_block(owner)) for owner in (chip, *plane)]
    x_slots, x_own = x_state
    x_own.wait()
    links.waits = [item for item in links.waits if item[0] is not x_own]
    x_chains[0].start(0)

    set_out(2)

    gain_second = gains_ref[1:2, :].astype(F32)
    router = qkvw[pl.ds(2 * n, 2), :, 1536:1664].reshape(part_width, 128)
    logit_part = mm(router, (middle * gain_second).astype(BF), ((0,), (1,)))[0:8, :]
    square = middle * middle
    square_high = square.astype(BF)
    square_low = (square - square_high.astype(F32)).astype(BF)
    ones = jnp.ones((8, part_width), BF)
    square_sum = rows_rows(ones, square_high) + rows_rows(ones, square_low)
    stat = jnp.where(kind == 4, square_sum, logit_part)
    stat_send[...] = stat
    stat_slots = [links.slot() for _ in range(NEAR)]
    for step in range(NEAR):
        links.send(stat_send, stat_recv.at[step], {"narrow": to_z[step]}, stat_slots[step])

    for step in range(NEAR):
        links.land(slot_block(x_out, plane[step]), at_plane(plane[step]), x_slots[step])
        x_chains[1 + step].start(0)
    for step in range(NEAR):
        links.land(stat_recv.at[step], {"narrow": from_z[step]}, stat_slots[step])
        stat = stat + stat_recv[step]
    stat_out[...] = stat
    scale_row = lax.rsqrt(stat[4:5, :] * (1.0 / (4 * part_width)) + NORM_EPS)
    logits = jnp.where(kind < EXPERTS, stat * scale_row, NEG_FILL)
    chances = jnp.exp(logits - jnp.max(logits, 0, keepdims=True))
    chances = chances / jnp.sum(chances, 0, keepdims=True)
    share_first = jnp.sum(chances * hot_first, 0, keepdims=True)
    share_second = jnp.sum(chances * hot_second, 0, keepdims=True)
    both = share_first + share_second
    weighted = pick_first * (share_first / both) + pick_second * (share_second / both)
    slot_gate = jnp.sum(weighted, 1, keepdims=True)
    gate_send[...] = jnp.broadcast_to(slot_gate, (SLOTS, 128))

    def gate_rows(array, owner):
        return array.at[pl.ds(pl.multiple_of(owner * CAP, 16), CAP), :]

    gate_slots = [links.slot() for _ in range(NEAR)]
    for step in range(NEAR):
        links.send(
            gate_rows(gate_send, plane[step]), gate_rows(gate_out, chip),
            at_plane(plane[step]), gate_slots[step],
        )
    links.move(gate_rows(gate_send, chip), gate_rows(gate_out, chip))

    for step in range(2):
        for chain in x_chains:
            chain.land(step)
            chain.start(step + 1)
        pass_on(step)
    for chain in x_chains:
        chain.land(2)
    dy_chain.land(2)
    for step in range(NEAR):
        links.land(gate_rows(gate_out, plane[step]), at_plane(plane[step]), gate_slots[step])
    pass_on(2)
    for kind_at in range(3):
        all_there(kind_at)
    links.finish()


def front_call(tokens, cotangent, gains, weights, router, experts, segment, parents, ids, rank):
    token_count, part_width = tokens.shape
    full = 4 * part_width
    rows_each, _, hidden_width = experts[0].shape
    heads = part_width // HEAD_DIM
    vmem = pl.BlockSpec(memory_space=pltpu.VMEM)
    hbm = pl.BlockSpec(memory_space=pl.ANY)

    def arr(shape, dtype):
        return jax.ShapeDtypeStruct(shape, dtype)

    return pl.pallas_call(
        front_body,
        out_shape=(
            arr((8, rows_each, 1664), BF),
            arr((8, rows_each, part_width), BF),
            arr((3, 4, 2, rows_each, hidden_width), BF),
            arr((SLOTS, full), BF),
            arr((SLOTS, full), BF),
            arr((SLOTS, 128), F32),
            arr((token_count, part_width), F32),
            arr((token_count, full), BF),
            arr((4, token_count + 16, part_width), BF),
            arr((3, token_count, part_width), BF),
            arr((heads, token_count, token_count), F32),
            arr((token_count, part_width), BF),
            arr((8, token_count), F32),
            arr((2, token_count, HEAD_DIM), F32),
            arr((2, SLOTS, token_count), BF),
            arr((token_count, 128), F32),
        ),
        in_specs=[vmem] * 8 + [hbm] * 3 + [vmem] * 4,
        out_specs=(hbm, hbm, hbm) + (vmem,) * 13,
        scratch_shapes=[
            pltpu.VMEM((3, token_count, part_width), F32),
            pltpu.VMEM((token_count, token_count), F32),
            pltpu.VMEM((3, rows_each, EXPERTS, hidden_width), BF),
            pltpu.VMEM((3, EXPERTS, rows_each, hidden_width), BF),
            pltpu.VMEM((rows_each, 1664), BF),
            pltpu.VMEM((token_count + 16, part_width), BF),
            pltpu.VMEM((8, rows_each, 1664), BF),
            pltpu.VMEM((8, rows_each, part_width), BF),
            pltpu.VMEM((SLOTS, part_width), BF),
            pltpu.VMEM((SLOTS, part_width), BF),
            pltpu.VMEM((NEAR, token_count, part_width), BF),
            pltpu.VMEM((NEAR + 1, token_count, part_width), BF),
            pltpu.VMEM((8, token_count), F32),
            pltpu.VMEM((NEAR, 8, token_count), F32),
            pltpu.VMEM((SLOTS, 128), F32),
            pltpu.SemaphoreType.DMA((FRONT_SLOTS,)),
            pltpu.SemaphoreType.DMA((FRONT_SLOTS,)),
            pltpu.SemaphoreType.DMA((16,)),
        ],
        compiler_params=pltpu.CompilerParams(
            collective_id=0, has_side_effects=True, vmem_limit_bytes=60 * 1024 * 1024
        ),
        cost_estimate=pl.CostEstimate(
            flops=6_000_000_000, bytes_accessed=60_000_000, transcendentals=400_000
        ),
        name="front",
    )(tokens, cotangent, gains, *weights, router, *experts, segment, parents, ids, rank)


MID_SLOTS = 48


TILE = 512


def mid_body(
    x_ref, dy_ref, gate_ref, tokens_ref, w_ref,
    back_mid_out, back_exp_out, last_exp_out, extra_out, grads_out, expert_out,
    weights, hidden, graded_send, hidden_cat, graded_cat, act_cat, gate_cat, up_cat,
    turned, down_grad, rs_send, rs_recv, ext_send, ext_recv, sent, landed, local,
):
    n = lax.axis_index("narrow")
    w = lax.axis_index("wide")
    chip, core = w // 2, lax.rem(w, 2)
    to_z, from_z = places_of(n)
    plane = plane_of(chip)
    links = Links(sent, landed, local)
    mate = {"wide": 2 * chip + 1 - core}
    slots, full = hidden.shape
    part_width = full // 4
    rows_each = full // 8
    half = full // 2
    hidden_width = weights.shape[2]

    x_load = links.move(x_ref, hidden)
    loads = [
        links.move(
            w_ref.at[kind, c, k],
            weights.at[kind, pl.ds((2 * c + k) * rows_each, rows_each), :],
        )
        for kind in range(3)
        for c in range(4)
        for k in range(2)
    ]
    links.waits = []
    greet(to_z, plane, chip, core, True)

    slot_gate = gate_ref[:, 0:1]
    for c in range(4):
        theirs = pl.ds(pl.multiple_of((2 * c + 1 - core) * rows_each, rows_each), rows_each)
        ours = pl.ds(pl.multiple_of((2 * c + core) * rows_each, rows_each), rows_each)
        cols = slice(c * rows_each, (c + 1) * rows_each)
        graded_cat[core, :, cols] = (dy_ref[:, ours].astype(F32) * slot_gate).astype(BF)
        graded_send[:, cols] = (dy_ref[:, theirs].astype(F32) * slot_gate).astype(BF)

    def to_mate(source, target):
        slot = links.slot()
        links.send(source, target.at[core], mate, slot)
        return lambda: links.land(target.at[1 - core], mate, slot)

    graded_there = to_mate(graded_send, graded_cat)
    x_load.wait()
    total = jnp.zeros((slots, 1), F32)
    for m in range(4):
        part = hidden[:, m * part_width : (m + 1) * part_width].astype(F32)
        total = total + jnp.sum(part * part, 1, keepdims=True)
    scale = lax.rsqrt(total * (1.0 / full) + NORM_EPS)
    gain_row = tokens_ref.shape[1] - 15
    for m in range(4):
        cols = slice(m * part_width, (m + 1) * part_width)
        gain = tokens_ref[m, gain_row : gain_row + 1, :].astype(F32)
        hidden[:, cols] = (hidden[:, cols].astype(F32) * scale * gain).astype(BF)
    hidden_slots = [links.slot() for _ in range(4)]
    for c in range(4):
        cols = pl.ds(c * rows_each, rows_each)
        theirs = pl.ds(pl.multiple_of((2 * c + 1 - core) * rows_each, rows_each), rows_each)
        ours = pl.ds(pl.multiple_of((2 * c + core) * rows_each, rows_each), rows_each)
        links.send(hidden.at[:, theirs], hidden_cat.at[core, :, cols], mate, hidden_slots[c])
        hidden_cat[core, :, c * rows_each : (c + 1) * rows_each] = hidden[:, ours]
    for load in loads:
        load.wait()

    def one_tile(cols, rows):
        gate_pre = low_dot(hidden[rows, :], weights[0, :, cols])
        up_pre = low_dot(hidden[rows, :], weights[1, :, cols])
        act_raw = low_dot(dy_ref[rows, :], weights[2, :, cols])
        sigmoid = 1.0 / (1.0 + jnp.exp(-gate_pre))
        silu = gate_pre * sigmoid
        activated = (silu * up_pre).astype(BF)
        grad_act = act_raw * gate_ref[rows, 0:1]
        act_cat[core, rows, cols] = activated
        gate_cat[core, rows, cols] = (
            grad_act * up_pre * (sigmoid * (1.0 + gate_pre * (1.0 - sigmoid)))
        ).astype(BF)
        up_cat[core, rows, cols] = (grad_act * silu).astype(BF)
        return jnp.sum(act_raw * activated.astype(F32), 1, keepdims=True)

    def over_tiles(tile, body, carry):
        whole = hidden_width // tile
        carry = lax.fori_loop(
            0, whole, lambda t, value: body(pl.ds(pl.multiple_of(t * tile, tile), tile), value), carry
        )
        if hidden_width % tile:
            carry = body(pl.ds(whole * tile, hidden_width % tile), carry)
        return carry

    share = over_tiles(
        TILE,
        lambda cols, value: tuple(
            value[index] + one_tile(cols, pl.ds(index * (slots // 2), slots // 2))
            for index in range(2)
        ),
        (jnp.zeros((slots // 2, 1), F32),) * 2,
    )
    share = jnp.concatenate(share, 0)
    acts_there = [to_mate(item.at[core], item) for item in (act_cat, gate_cat, up_cat)]

    grad_gate, grad_up = gate_cat.at[core], up_cat.at[core]
    mid_sum = LineSum(links, n, rs_send.at[0], rs_recv.at[0])

    def mid_part(owner):
        rows = pl.ds(pl.multiple_of(owner * part_width, part_width), part_width)
        block = rows_rows(grad_gate[...], weights[0, rows, :])
        block = block + rows_rows(grad_up[...], weights[1, rows, :])
        return block, jnp.sum(hidden[:, rows].astype(F32) * block, 1, keepdims=True)

    stat = jnp.zeros((slots, 1), F32)
    block, part = mid_part(mid_sum.targets[0])
    mid_sum.put(0, block)
    stat = stat + part

    expert_slots = {}

    def weight_grad(right, target):
        def body(cols, value):
            right_rows = right[:, :, cols].reshape(2 * slots, cols.size)
            target[:, cols] = low_dot(turned[...], right_rows).astype(BF)
            return value

        over_tiles(TILE, body, 0)

    def share_out(index, source):
        expert_slots[index] = [links.slot() for _ in range(NEAR)]

        def block(owner):
            first = pl.multiple_of(owner * rows_each, rows_each)
            return source.at[pl.ds(first, rows_each), :]

        for step in range(NEAR):
            links.send(
                block(plane[step]), expert_out.at[index, chip],
                {"wide": 2 * plane[step] + core}, expert_slots[index][step],
            )
        links.move(block(chip), expert_out.at[index, chip])

    graded_there()
    acts_there[0]()
    turned[...] = graded_cat[...].reshape(2 * slots, half).T
    weight_grad(act_cat, down_grad)
    share_out(0, down_grad)

    def other_part(step, stat):
        block, part = mid_part(mid_sum.owner(step))
        rs_send[0, step] = block.astype(BF)
        return stat + part

    stat = lax.fori_loop(1, 4, other_part, stat)
    mid_sum.set_out(1)
    mid_sum.set_out(2)
    lane_at = lax.broadcasted_iota(jnp.int32, (slots, 128), 1)
    columns = jnp.where(lane_at == 0, share, jnp.where(lane_at == 1, stat, 0.0))
    high = columns.astype(BF)
    rest = (columns - high.astype(F32)).astype(BF)
    pick = jnp.where(
        lax.broadcasted_iota(jnp.int32, (8, 128), 0) == lax.broadcasted_iota(jnp.int32, (8, 128), 1),
        1.0, 0.0,
    ).astype(BF)
    extra = rows_rows(pick, high) + rows_rows(pick, rest)
    ext_send[...] = extra
    ext_slots = [links.slot() for _ in range(NEAR)]
    for step in range(NEAR):
        links.send(ext_send, ext_recv.at[step], {"narrow": to_z[step]}, ext_slots[step])

    mid_sum.relay()

    activated = act_cat.at[core]
    exp_sum = LineSum(links, n, rs_send.at[1], rs_recv.at[1])

    def exp_part(owner):
        rows = pl.ds(pl.multiple_of(owner * part_width, part_width), part_width)
        return rows_rows(activated[...], weights[2, rows, :])

    def expert_part(step, value):
        rs_send[1, step] = exp_part(exp_sum.owner(step)).astype(BF)
        return value

    lax.fori_loop(0, 4, expert_part, 0)
    exp_sum.set_out(0)
    exp_sum.set_out(1)
    for slot in hidden_slots:
        index = hidden_slots.index(slot)
        links.land(
            hidden_cat.at[1 - core, :, pl.ds(index * rows_each, rows_each)], mate, slot
        )
    for there in acts_there[1:]:
        there()
    turned[...] = hidden_cat[...].reshape(2 * slots, half).T
    gate_grad = weights.at[0, pl.ds(0, half), :]
    weight_grad(gate_cat, gate_grad)
    share_out(1, gate_grad)
    up_grad = weights.at[1, pl.ds(0, half), :]
    weight_grad(up_cat, up_grad)
    links.move(up_grad, grads_out)

    for step in range(NEAR):
        links.land(ext_recv.at[step], {"narrow": from_z[step]}, ext_slots[step])
        extra = extra + ext_recv[step]
    high = extra.astype(BF)
    rest = (extra - high.astype(F32)).astype(BF)
    place = lax.broadcasted_iota(jnp.int32, (8, 128), 0) * 2
    lanes = lax.broadcasted_iota(jnp.int32, (8, 128), 1)
    spread_high = jnp.where(place == lanes, 1.0, 0.0).astype(BF)
    spread_low = jnp.where(place + 1 == lanes, 1.0, 0.0).astype(BF)
    columns = mm(high, spread_high, ((0,), (0,))) + mm(rest, spread_low, ((0,), (0,)))
    extra_out[...] = jnp.where(lane_at == 4, 1.0, columns).astype(BF)
    back_mid_out[...] = mid_sum.total(rs_send[0, 3].astype(F32)).astype(BF)
    exp_sum.join()
    last_exp_out[...] = rs_send[1, 2]
    back_exp_out[...] = exp_sum.early(rs_send[1, 3].astype(F32)).astype(BF)
    for index in range(2):
        for step in range(NEAR):
            links.land(
                expert_out.at[index, plane[step]], {"wide": 2 * plane[step] + core},
                expert_slots[index][step],
            )
    links.finish()


def mid_call(slot_mid, slot_grad, slot_gate, token_parts, expert_w):
    slots, full = slot_mid.shape
    part_width = full // 4
    rows_each, hidden_width = expert_w.shape[3:]
    vmem = pl.BlockSpec(memory_space=pltpu.VMEM)
    hbm = pl.BlockSpec(memory_space=pl.ANY)

    def arr(shape, dtype):
        return jax.ShapeDtypeStruct(shape, dtype)

    return pl.pallas_call(
        mid_body,
        out_shape=(
            arr((slots, part_width), BF),
            arr((slots, part_width), BF),
            arr((slots, part_width), BF),
            arr((slots, 128), BF),
            arr((full // 2, hidden_width), BF),
            arr((2, 4, rows_each, hidden_width), BF),
        ),
        in_specs=[hbm] + [vmem] * 3 + [hbm],
        out_specs=(vmem,) * 4 + (hbm, hbm),
        scratch_shapes=[
            pltpu.VMEM((3, full, hidden_width), BF),
            pltpu.VMEM((slots, full), BF),
            pltpu.VMEM((slots, full // 2), BF),
            pltpu.VMEM((2, slots, full // 2), BF),
            pltpu.VMEM((2, slots, full // 2), BF),
            pltpu.VMEM((2, slots, hidden_width), BF),
            pltpu.VMEM((2, slots, hidden_width), BF),
            pltpu.VMEM((2, slots, hidden_width), BF),
            pltpu.VMEM((full // 2, 2 * slots), BF),
            pltpu.VMEM((full // 2, hidden_width), BF),
            pltpu.VMEM((2, NEAR + 1, slots, part_width), BF),
            pltpu.VMEM((2, NEAR + 1, slots, part_width), BF),
            pltpu.VMEM((8, slots), F32),
            pltpu.VMEM((NEAR, 8, slots), F32),
            pltpu.SemaphoreType.DMA((MID_SLOTS,)),
            pltpu.SemaphoreType.DMA((MID_SLOTS,)),
            pltpu.SemaphoreType.DMA((32,)),
        ],
        compiler_params=pltpu.CompilerParams(
            collective_id=1, has_side_effects=True, vmem_limit_bytes=62 * 1024 * 1024
        ),
        cost_estimate=pl.CostEstimate(
            flops=30_000_000_000, bytes_accessed=40_000_000, transcendentals=800_000
        ),
        name="mid",
    )(slot_mid, slot_grad, slot_gate, token_parts, expert_w)


class PlaneSum:
    def __init__(self, links, core, chip, plane, first, send, inbox):
        self.links, self.core, self.chip = links, core, chip
        self.near, self.next, self.far = plane[first], plane[1 - first], plane[2]
        self.send, self.inbox = send, inbox
        self.slots = [links.slot() for _ in range(3)]

    def at(self, peer):
        return {"wide": 2 * peer + self.core}

    def block(self, owner):
        rows = self.inbox.shape[1]
        return self.send.at[pl.ds(pl.multiple_of(owner * rows, rows), rows), :]

    def start(self):
        links = self.links
        links.send(self.block(self.far), self.inbox.at[1], self.at(self.near), self.slots[1])
        links.send(self.block(self.near), self.inbox.at[0], self.at(self.near), self.slots[0])

    def turn(self):
        links = self.links
        links.land(self.inbox.at[1], self.at(self.near), self.slots[1])
        block = self.block(self.next)
        block[...] = (block[...].astype(F32) + self.inbox[1].astype(F32)).astype(BF)
        links.send(block, self.inbox.at[2], self.at(self.next), self.slots[2])

    def total(self):
        links = self.links
        links.land(self.inbox.at[0], self.at(self.near), self.slots[0])
        links.land(self.inbox.at[2], self.at(self.next), self.slots[2])
        own = self.block(self.chip)[...].astype(F32)
        return own + self.inbox[0].astype(F32) + self.inbox[2].astype(F32)


TAIL_SLOTS = 72


def tail_body(
    mid_ref, exp_ref, last_ref, ext_ref, moved_ref, picks_ref, stat_ref, cols_ref, middle_ref, cot_ref,
    tok_ref, tokens_ref, qkv_ref, prob_ref, att_ref, rope_ref, hidden_ref, qkvw_ref, outw_ref,
    output_out, grad_tokens_out, summed_out, small_out,
    router_out, expert_out,
    grad_att_at, exp_in, exp_sum, router_all, qkvw, outw, ret_mid, ret_exp, ret_ext, branch, hidden_cat, branch_cat, att_cat, proj_cat,
    proj_send, proj_recv, first_send, first_recv, col_send, col_recv, small_mate, small_sum,
    small_recv, last_mate, last_sum, last_recv, sent, landed, local,
):
    n = lax.axis_index("narrow")
    w = lax.axis_index("wide")
    chip, core = w // 2, lax.rem(w, 2)
    to_z, from_z = places_of(n)
    plane = plane_of(chip)
    links = Links(sent, landed, local)
    mate = {"wide": 2 * chip + 1 - core}
    token_count, part_width = tok_ref.shape
    full = 4 * part_width
    rows_each = full // 8
    heads = part_width // HEAD_DIM
    half = full // 2

    def at_plane(peer):
        return {"wide": 2 * peer + core}

    def cap_rows(array, owner):
        return array.at[pl.ds(pl.multiple_of(owner * CAP, 16), CAP), :]

    loads = [links.move(qkvw_ref, qkvw), links.move(outw_ref, outw)]
    links.waits = []
    greet(to_z, plane, chip, core, True)

    last_slot = links.slot()
    links.send(last_ref, exp_in, {"narrow": lax.rem(2 * n + 1, 5)}, last_slot)

    back_slots = []

    def give_back(source, target):
        slots = [links.slot() for _ in range(NEAR)]
        for step in range(NEAR):
            links.send(
                cap_rows(source, plane[step]), cap_rows(target, chip), at_plane(plane[step]),
                slots[step],
            )
        own = links.move(cap_rows(source, chip), cap_rows(target, chip))
        links.waits.pop()
        back_slots.append((target, slots, own))

    give_back(mid_ref, ret_mid)
    give_back(ext_ref, ret_ext)

    def returned(which):
        target, slots, own = back_slots[which]
        for step in range(NEAR):
            links.land(cap_rows(target, plane[step]), at_plane(plane[step]), slots[step])
        own.wait()
        return target[...]

    expert_slots = [links.slot() for _ in range(NEAR)]
    for step in range(NEAR):
        block = pl.ds(pl.multiple_of(plane[step] * rows_each, rows_each), rows_each)
        links.send(
            moved_ref.at[block, :], expert_out.at[chip], at_plane(plane[step]), expert_slots[step]
        )
    block = pl.ds(pl.multiple_of(chip * rows_each, rows_each), rows_each)
    links.move(moved_ref.at[block, :], expert_out.at[chip])

    def to_mate(source, target):
        slot = links.slot()
        links.send(source, target.at[core], mate, slot)
        return lambda: links.land(target.at[1 - core], mate, slot)

    def parity_exchange(source, target):
        lands = []
        for c in range(4):
            cols = pl.ds(c * rows_each, rows_each)
            theirs = pl.ds(pl.multiple_of((2 * c + 1 - core) * rows_each, rows_each), rows_each)
            ours = pl.ds(pl.multiple_of((2 * c + core) * rows_each, rows_each), rows_each)
            slot = links.slot()
            links.send(source.at[:, theirs], target.at[core, :, cols], mate, slot)
            target[core, :, c * rows_each : (c + 1) * rows_each] = source[:, ours]
            lands.append((target.at[1 - core, :, cols], slot))
        return lambda: [links.land(block, mate, slot) for block, slot in lands]

    hidden_there = parity_exchange(hidden_ref, hidden_cat)
    att_cat[core] = att_ref[...]
    att_there = to_mate(att_ref, att_cat)

    stat = jnp.concatenate([stat_ref[...], jnp.zeros((120, token_count), F32)], 0).T
    lane_at = lax.broadcasted_iota(jnp.int32, (token_count, 128), 1)
    scale_second = lax.rsqrt(stat[:, 4:5] * (1.0 / full) + NORM_EPS)
    logits = stat * scale_second
    hot_first = lane_at == cols_ref[:, 2:3].astype(jnp.int32)
    hot_second = lane_at == cols_ref[:, 3:4].astype(jnp.int32)
    logit_first = jnp.sum(jnp.where(hot_first, logits, 0.0), 1, keepdims=True)
    logit_second = jnp.sum(jnp.where(hot_second, logits, 0.0), 1, keepdims=True)
    apart = logit_first - logit_second
    share_first = 1.0 / (1.0 + jnp.exp(-apart))
    share_second = 1.0 / (1.0 + jnp.exp(apart))
    normed = middle_ref[...] * scale_second
    gain_second = tokens_ref[n, token_count + 1 : token_count + 2, :].astype(F32)
    hidden_second = (normed * gain_second).astype(BF)
    for load in loads:
        load.wait()
    router = qkvw[pl.ds(2 * n, 2), :, 1536:1664].reshape(part_width, 128)

    rows_mid = returned(0)
    rows_ext = returned(1)
    ext_first = cols_cols(picks_ref[0], rows_ext)
    ext_second = cols_cols(picks_ref[1], rows_ext)
    ext_both = ext_first + ext_second
    grad_share = ext_first[:, 0:1] + ext_first[:, 1:2] - ext_second[:, 0:1] - ext_second[:, 1:2]
    delta = (grad_share * share_first * share_second).astype(BF).astype(F32)
    grad_logits = jnp.where(hot_first, delta, jnp.where(hot_second, -delta, 0.0)).astype(BF)
    stat_total = ext_both[:, 2:3] + ext_both[:, 3:4] + delta * apart
    grad_hidden = cols_cols(picks_ref[0] + picks_ref[1], rows_mid) + rows_rows(grad_logits, router)
    grad_middle = cot_ref[...].astype(F32) + scale_second * (
        gain_second * grad_hidden - normed * (stat_total * (1.0 / full))
    )
    own_cols = pl.ds(pl.multiple_of(n * part_width, part_width), part_width)
    branch[:, own_cols] = grad_middle.astype(BF)
    branch_slots = [links.slot() for _ in range(NEAR)]
    for step in range(NEAR):
        links.send(
            branch.at[:, own_cols], branch.at[:, own_cols], {"narrow": to_z[step]},
            branch_slots[step],
        )

    links.land(exp_in, {"narrow": lax.rem(n + 1, 4)}, last_slot)
    exp_sum[...] = (exp_ref[...].astype(F32) + exp_in[...].astype(F32)).astype(BF)
    give_back(exp_sum, ret_exp)

    router_part = cols_cols(grad_logits, hidden_second)[0:8, :]
    gain_part = jnp.sum(grad_hidden * normed, 0, keepdims=True)
    kind_at = lax.broadcasted_iota(jnp.int32, (8, part_width), 0)
    small = jnp.where(kind_at == 4, gain_part, router_part)
    small_mate[core] = small
    small_there = to_mate(small_mate.at[core], small_mate)

    small_there()
    small = small_mate[0] + small_mate[1]
    small_sum[...] = small
    small_slots = [links.slot() for _ in range(NEAR)]
    for step in range(NEAR):
        links.send(small_sum, small_recv.at[step], at_plane(plane[step]), small_slots[step])

    for step in range(NEAR):
        cols = pl.ds(pl.multiple_of(from_z[step] * part_width, part_width), part_width)
        links.land(branch.at[:, cols], {"narrow": from_z[step]}, branch_slots[step])
    branch_there = parity_exchange(branch, branch_cat)
    grad_att = low_dot(branch[...], outw[...].reshape(full, part_width)).astype(BF)

    proj_sums = {
        part: PlaneSum(
            links, core, chip, plane, part % 2, proj_send.at[part], proj_recv.at[part]
        )
        for part in (3, 0, 1, 2)
    }

    branch_there()
    att_there()
    proj_send[3] = cols_cols(
        branch_cat[...].reshape(2 * token_count, half), att_cat[...].reshape(2 * token_count, part_width)
    ).astype(BF)
    proj_sums[3].start()
    score_scale = HEAD_DIM ** (-0.5)
    grad_att_at[...] = grad_att

    def one_head(head, stat_first):
        def lanes(start):
            return pl.ds(pl.multiple_of(start + head * HEAD_DIM, HEAD_DIM), HEAD_DIM)

        query, key, value = (qkv_ref[i, :, lanes(0)] for i in range(3))
        grad_out = grad_att_at[:, lanes(0)]
        weights = prob_ref[head]
        grad_weights = rows_rows(grad_out, value)
        inner = jnp.sum(weights * grad_weights, 1, keepdims=True)
        grad_scores = (weights * (grad_weights - inner)).astype(BF)
        grad_query = low_dot(grad_scores, key) * score_scale
        grad_key = cols_cols(grad_scores, query) * score_scale
        grad_value = cols_cols(weights.astype(BF), grad_out)
        products = (
            grad_query * query.astype(F32)
            + grad_key * key.astype(F32)
            + grad_value * value.astype(F32)
        )
        for part, grad in ((0, grad_query), (1, grad_key)):
            turned = grad * rope_ref[0] - pltpu.roll(grad, HEAD_DIM // 2, 1) * rope_ref[1]
            proj_cat[core, :, lanes(part * part_width)] = turned.astype(BF)
        proj_cat[core, :, lanes(2 * part_width)] = grad_value.astype(BF)
        return stat_first + jnp.sum(products, 1, keepdims=True)

    stat_first = lax.fori_loop(0, heads, one_head, jnp.zeros((token_count, 1), F32))
    proj_there = to_mate(proj_cat.at[core], proj_cat)
    high = stat_first.astype(BF)
    rest = (stat_first - high.astype(F32)).astype(BF)
    col_send[...] = jnp.where(
        lane_at == 0, high.astype(F32), jnp.where(lane_at == 1, rest.astype(F32), 0.0)
    ).astype(BF)
    col_slots = [links.slot() for _ in range(NEAR)]
    for step in range(NEAR):
        links.send(col_send, col_recv.at[step], {"narrow": to_z[step]}, col_slots[step])
    grads = proj_cat[core]

    def first_block(m):
        weight = qkvw[pl.ds(2 * m, 2), :, 0:1536].reshape(part_width, 1536)
        return rows_rows(grads, weight)

    def fill_first(step, value):
        first_send[step] = first_block(lax.rem(n + 1 + step, 4)).astype(BF)
        return value

    lax.fori_loop(0, NEAR, fill_first, 0)
    first_slots = [links.slot() for _ in range(NEAR)]
    for step in range(NEAR):
        links.send(
            first_send.at[step], first_recv.at[step], {"narrow": to_z[step]}, first_slots[step]
        )

    hidden_there()
    proj_there()
    hidden_rows = hidden_cat[...].reshape(2 * token_count, half)
    proj_sums[3].turn()
    for part in range(3):
        cols = slice(part * 512, (part + 1) * 512)
        proj_send[part] = cols_cols(
            hidden_rows, proj_cat[:, :, cols].reshape(2 * token_count, part_width)
        ).astype(BF)
        proj_sums[part].start()

    rows_exp = returned(2)
    output_out[...] = (
        middle_ref[...]
        + share_first * cols_cols(picks_ref[0], rows_exp)
        + share_second * cols_cols(picks_ref[1], rows_exp)
    ).astype(BF)

    grad_first = first_block(n)
    stat_first = high.astype(F32) + rest.astype(F32)
    total = jnp.zeros((token_count, 1), F32)
    for m in range(4):
        part = tokens_ref[m, 0:token_count, :].astype(F32)
        total = total + jnp.sum(part * part, 1, keepdims=True)
    scale_first = lax.rsqrt(total * (1.0 / full) + NORM_EPS)
    normed_first = tok_ref[...].astype(F32) * scale_first
    gain_first = tokens_ref[n, token_count : token_count + 1, :].astype(F32)
    for step in range(NEAR):
        links.land(col_recv.at[step], {"narrow": from_z[step]}, col_slots[step])
        stat_first = stat_first + (
            col_recv[step, :, 0:1].astype(F32) + col_recv[step, :, 1:2].astype(F32)
        )
    for step in range(NEAR):
        links.land(first_recv.at[step], {"narrow": from_z[step]}, first_slots[step])
        grad_first = grad_first + first_recv[step].astype(F32)
    grad_tokens_out[...] = grad_middle + scale_first * (
        gain_first * grad_first - normed_first * (stat_first * (1.0 / full))
    )
    gain_part = jnp.sum(grad_first * normed_first, 0, keepdims=True)
    for part in range(3):
        proj_sums[part].turn()
    last_mate[core] = jnp.broadcast_to(gain_part, (8, part_width))
    last_there = to_mate(last_mate.at[core], last_mate)

    for step in range(NEAR):
        links.land(small_recv.at[step], at_plane(plane[step]), small_slots[step])
        small = small + small_recv[step]
    last_there()
    last = last_mate[0] + last_mate[1]
    last_sum[...] = last
    last_slots = [links.slot() for _ in range(NEAR)]
    for step in range(NEAR):
        links.send(last_sum, last_recv.at[step], at_plane(plane[step]), last_slots[step])
    router_all[:, own_cols] = small
    router_slots = [links.slot() for _ in range(NEAR)]
    for step in range(NEAR):
        links.send(
            router_all.at[:, own_cols], router_all.at[:, own_cols], {"narrow": to_z[step]},
            router_slots[step],
        )
    for step in range(NEAR):
        links.land(last_recv.at[step], at_plane(plane[step]), last_slots[step])
        last = last + last_recv[step]
    small_out[...] = jnp.where(kind_at == 5, last, small)
    for step in range(NEAR):
        cols = pl.ds(pl.multiple_of(from_z[step] * part_width, part_width), part_width)
        links.land(router_all.at[:, cols], {"narrow": from_z[step]}, router_slots[step])

    router_out[...] = router_all[:, pl.ds(pl.multiple_of(w * rows_each, rows_each), rows_each)]
    for part in range(4):
        summed_out[:, part * part_width : (part + 1) * part_width] = proj_sums[part].total()
    for step in range(NEAR):
        links.land(expert_out.at[plane[step]], at_plane(plane[step]), expert_slots[step])
    links.finish()


def tail_call(*args):
    slots, part_width = args[0].shape
    half, hidden_width = args[4].shape
    token_count = args[10].shape[0]
    full, rows_each = 2 * half, half // 4
    vmem = pl.BlockSpec(memory_space=pltpu.VMEM)
    hbm = pl.BlockSpec(memory_space=pl.ANY)

    def arr(shape, dtype):
        return jax.ShapeDtypeStruct(shape, dtype)

    own = (token_count, part_width)
    return pl.pallas_call(
        tail_body,
        out_shape=(
            arr(own, BF),
            arr(own, F32),
            arr((rows_each, full), F32),
            arr((8, part_width), F32),
            arr((8, rows_each), F32),
            arr((4, rows_each, hidden_width), BF),
        ),
        in_specs=[vmem] * 4 + [hbm] + [vmem] * 12 + [hbm] * 2,
        out_specs=(vmem,) * 5 + (hbm,),
        scratch_shapes=[
            pltpu.VMEM(own, BF),
            pltpu.VMEM((slots, part_width), BF),
            pltpu.VMEM((slots, part_width), BF),
            pltpu.VMEM((8, full), F32),
            pltpu.VMEM((8, rows_each, 1664), BF),
            pltpu.VMEM((8, rows_each, part_width), BF),
            pltpu.VMEM((slots, part_width), BF),
            pltpu.VMEM((slots, part_width), BF),
            pltpu.VMEM((slots, 128), BF),
            pltpu.VMEM((token_count, full), BF),
            pltpu.VMEM((2, token_count, half), BF),
            pltpu.VMEM((2, token_count, half), BF),
            pltpu.VMEM((2, token_count, part_width), BF),
            pltpu.VMEM((2, token_count, 1536), BF),
            pltpu.VMEM((4, half, part_width), BF),
            pltpu.VMEM((4, NEAR, rows_each, part_width), BF),
            pltpu.VMEM((NEAR,) + own, BF),
            pltpu.VMEM((NEAR,) + own, BF),
            pltpu.VMEM((token_count, 128), BF),
            pltpu.VMEM((NEAR, token_count, 128), BF),
            pltpu.VMEM((2, 8, part_width), F32),
            pltpu.VMEM((8, part_width), F32),
            pltpu.VMEM((NEAR, 8, part_width), F32),
            pltpu.VMEM((2, 8, part_width), F32),
            pltpu.VMEM((8, part_width), F32),
            pltpu.VMEM((NEAR, 8, part_width), F32),
            pltpu.SemaphoreType.DMA((TAIL_SLOTS,)),
            pltpu.SemaphoreType.DMA((TAIL_SLOTS,)),
            pltpu.SemaphoreType.DMA((16,)),
        ],
        compiler_params=pltpu.CompilerParams(
            collective_id=2, has_side_effects=True, vmem_limit_bytes=60 * 1024 * 1024
        ),
        cost_estimate=pl.CostEstimate(
            flops=6_000_000_000, bytes_accessed=60_000_000, transcendentals=1_000
        ),
        name="tail",
    )(*args)


def finish_body(
    down_ref, gate_ref, up_ref, output_ref, tokens_ref, summed_ref,
    gate_out, up_out, down_out, output_out, tokens_out, *proj_outs,
):
    def some_rows(index, value):
        rows = pl.ds(pl.multiple_of(index * 16, 16), 16)
        for source, target in ((gate_ref, gate_out), (up_ref, up_out), (down_ref, down_out)):
            for expert in range(EXPERTS):
                target[rows, expert, :] = source[expert, rows, :].astype(F32)
        return value

    lax.fori_loop(0, tokens_ref.shape[0] // 16, some_rows, 0)
    output_out[...] = output_ref[...]
    tokens_out[...] = tokens_ref[...]
    width = tokens_ref.shape[1]
    for part, target in enumerate(proj_outs):
        target[...] = summed_ref[:, part * width : (part + 1) * width].astype(F32)


def finish_call(early, late, output, grad_tokens, summed):
    _, rows_each, hidden_width = late.shape
    token_count, part_width = output.shape
    step = 32

    def flat(width):
        return pl.BlockSpec((step, width), lambda i: (i, 0))

    def cube(which):
        return pl.BlockSpec((None, EXPERTS, step, hidden_width), lambda i: (which, 0, i, 0))

    spread = pl.BlockSpec((step, EXPERTS, hidden_width), lambda i: (i, 0, 0))

    def arr(shape, dtype):
        return jax.ShapeDtypeStruct(shape, dtype)

    return pl.pallas_call(
        finish_body,
        grid=(rows_each // step,),
        out_shape=(arr((rows_each, EXPERTS, hidden_width), F32),) * 3
        + (arr(output.shape, BF), arr(output.shape, F32))
        + (arr((rows_each, part_width), F32),) * 4,
        in_specs=[
            cube(0), cube(1),
            pl.BlockSpec((EXPERTS, step, hidden_width), lambda i: (0, i, 0)),
            flat(part_width), flat(part_width), flat(4 * part_width),
        ],
        out_specs=(spread,) * 3 + (flat(part_width),) * 6,
        name="finish",
    )(early, early, late, output, grad_tokens, summed)


def plain_device(
    tokens, gain_attn, w_query, w_key, w_value, w_out, gain_ffn, w_router,
    w_gate, w_up, w_down, segment, parents, expert_ids, slot_order, cotangent,
):
    narrow_count = lax.axis_size("narrow")
    wide_count = lax.axis_size("wide")
    narrow_at = lax.axis_index("narrow")
    token_count, part_width = tokens.shape
    full_width = part_width * narrow_count
    hidden_width = w_gate.shape[2]
    rows_each = w_gate.shape[0]
    blocks = wide_count // 8
    quads = [
        [8 * block + 2 * chip + core for chip in range(4)]
        for block in range(blocks)
        for core in range(2)
    ]
    mates = [
        [8 * block + 2 * chip + core for block in range(blocks) for core in range(2)]
        for chip in range(4)
    ]

    def quad_swap(array):
        return lax.all_to_all(array, "wide", 0, 0, axis_index_groups=quads, tiled=True)

    def own_rows(weight):
        moved = quad_swap(jnp.transpose(weight, (1, 0, 2)))
        joined = lax.all_gather(moved, "wide", axis=0, axis_index_groups=mates, tiled=True)
        joined = joined.reshape(blocks, 2, 4, rows_each, hidden_width).transpose(0, 2, 1, 3, 4)
        return joined.reshape(full_width, hidden_width)

    def share_rows(grad):
        parts = grad.astype(BF).reshape(blocks, 4, 2, rows_each, hidden_width)
        parts = parts.transpose(0, 2, 1, 3, 4).reshape(blocks * 2, 4, rows_each, hidden_width)
        summed = lax.psum_scatter(
            parts, "wide", scatter_dimension=0, axis_index_groups=mates, tiled=True
        )[0]
        return jnp.transpose(quad_swap(summed), (1, 0, 2)).astype(F32)

    def head_cols(array, head):
        return array[:, head * HEAD_DIM : (head + 1) * HEAD_DIM]

    heads = part_width // HEAD_DIM
    half_dim = HEAD_DIM // 2
    freqs = ROPE_BASE ** (-2.0 * jnp.arange(half_dim, dtype=F32) / HEAD_DIM)
    score_scale = HEAD_DIM ** (-0.5)
    gains = jnp.stack([gain_attn, gain_ffn])
    gain_first_loc = gain_attn.astype(F32)
    gain_second_loc = gain_ffn.astype(F32)
    hot_first, hot_second, kept, pick_first, pick_second = route(expert_ids, slot_order[0])

    gate_w, up_w, down_w = own_rows(w_gate), own_rows(w_up), own_rows(w_down)
    attn_w = lax.all_gather(
        jnp.stack([w_query, w_key, w_value, w_out], 1), "wide", axis=0, tiled=True
    )
    query_w, key_w, value_w, out_w = (attn_w[:, i] for i in range(4))
    router_w = lax.all_gather(w_router, "wide", axis=0, tiled=True)
    tokens_full = lax.all_gather(tokens, "narrow", axis=1, tiled=True)
    grad_full = lax.all_gather(cotangent, "narrow", axis=1, tiled=True)
    gains_full = lax.all_gather(gains, "narrow", axis=1, tiled=True)
    gain_first = gains_full[0].astype(F32)
    gain_second = gains_full[1].astype(F32)

    seen, places = tree_layout(segment[0], parents[0])
    pick_first_low = pick_first.astype(BF)
    pick_second_low = pick_second.astype(BF)
    pick_both_low = (pick_first | pick_second).astype(BF)

    inputs_full = tokens_full.astype(F32)
    scale_first = lax.rsqrt(jnp.mean(inputs_full * inputs_full, -1, keepdims=True) + NORM_EPS)
    normed_first = inputs_full * scale_first
    hidden_first = (normed_first * gain_first).astype(BF)
    angles = places[:, None] * freqs[None, :]
    cosines, sines = jnp.cos(angles), jnp.sin(angles)
    query_raw = rows_cols(hidden_first, query_w)
    key_raw = rows_cols(hidden_first, key_w)
    value_low = rows_cols(hidden_first, value_w).astype(BF)

    saved = []
    outs = []
    for head in range(heads):
        query = rotate(head_cols(query_raw, head), cosines, sines).astype(BF)
        key = rotate(head_cols(key_raw, head), cosines, sines).astype(BF)
        value = head_cols(value_low, head)
        scores = jnp.where(seen, rows_rows(query, key) * score_scale, NEG_FILL)
        exps = jnp.exp(scores - jnp.max(scores, -1, keepdims=True))
        weights = exps / jnp.sum(exps, -1, keepdims=True)
        saved.append((query, key, value, weights))
        outs.append(rows_cols(weights.astype(BF), value).astype(BF))
    attended = jnp.concatenate(outs, 1)
    branch_part = rows_rows(attended, out_w).astype(BF)
    branch_loc = lax.psum_scatter(
        branch_part, "narrow", scatter_dimension=1, tiled=True
    ).astype(F32)
    middle = tokens.astype(F32) + branch_loc
    middle_full = lax.all_gather(middle.astype(BF), "narrow", axis=1, tiled=True).astype(F32)
    scale_second = lax.rsqrt(jnp.mean(middle_full * middle_full, -1, keepdims=True) + NORM_EPS)
    normed_second = middle_full * scale_second
    hidden_second = (normed_second * gain_second).astype(BF)
    logits = rows_cols(hidden_second, router_w)
    share_first, share_second = gate_pair(logits, hot_first, hot_second)
    weight_first = kept[:, 0] * share_first
    weight_second = kept[:, 1] * share_second

    slot_weight = jnp.sum(
        pick_first * weight_first[:, None] + pick_second * weight_second[:, None], 0
    )
    weight_high, weight_low = two_parts(slot_weight)
    pads = jnp.stack([weight_high, weight_low], 1)
    pads = jnp.pad(pads, ((0, 0), (0, 126)))
    sent_hidden = cols_cols(pick_both_low, hidden_second).astype(BF)
    sent_grad = cols_cols(pick_both_low, grad_full).astype(BF)
    sent = jnp.concatenate([sent_hidden, sent_grad, pads], 1)
    got = quad_swap(sent.reshape(EXPERTS, CAP, -1)).reshape(SLOTS, -1)
    slot_hidden = got[:, :full_width]
    slot_grad = got[:, full_width : 2 * full_width]
    slot_gate = got[:, 2 * full_width : 2 * full_width + 2].astype(F32)
    slot_gate = slot_gate[:, 0:1] + slot_gate[:, 1:2]

    gate_pre = rows_cols(slot_hidden, gate_w)
    up_pre = rows_cols(slot_hidden, up_w)
    sigmoid_gate = jax.nn.sigmoid(gate_pre)
    silu_gate = gate_pre * sigmoid_gate
    activated = (silu_gate * up_pre).astype(BF)
    expert_part = rows_rows(activated, down_w)
    act_raw = rows_cols(slot_grad, down_w)
    share_part = jnp.sum(act_raw * activated.astype(F32), 1, keepdims=True)
    grad_act = act_raw * slot_gate
    grad_gate_pre = (
        grad_act * up_pre * sigmoid_gate * (1.0 + gate_pre * (1.0 - sigmoid_gate))
    ).astype(BF)
    grad_up_pre = (grad_act * silu_gate).astype(BF)
    grad_slot = rows_rows(grad_gate_pre, gate_w) + rows_rows(grad_up_pre, up_w)
    stat_part = jnp.sum(slot_hidden.astype(F32) * grad_slot, 1, keepdims=True)
    extras = jnp.concatenate([*two_parts(share_part), *two_parts(stat_part)], 1)
    extras = jnp.pad(extras, ((0, 0), (0, 124)))
    back_parts = []
    expert_plain = expert_part.astype(BF)
    slot_plain = grad_slot.astype(BF)
    for part in range(narrow_count):
        cols = slice(part * part_width, (part + 1) * part_width)
        back_parts += [expert_plain[:, cols], slot_plain[:, cols], extras]
    back = lax.psum_scatter(
        jnp.concatenate(back_parts, 1), "narrow", scatter_dimension=1, tiled=True
    )
    back = quad_swap(back.reshape(EXPERTS, CAP, -1)).reshape(SLOTS, -1)
    picked_first = rows_cols(pick_first_low, back)
    picked_second = rows_cols(pick_second_low, back)
    output = (
        middle
        + weight_first[:, None] * picked_first[:, :part_width]
        + weight_second[:, None] * picked_second[:, :part_width]
    ).astype(BF)

    grad_weight = (slot_grad.astype(F32) * slot_gate).astype(BF)
    gate_out = share_rows(cols_cols(slot_hidden, grad_gate_pre))
    up_out = share_rows(cols_cols(slot_hidden, grad_up_pre))
    down_out = share_rows(cols_cols(grad_weight, activated))

    tail = 2 * part_width
    share_first_grad = picked_first[:, tail] + picked_first[:, tail + 1]
    share_second_grad = picked_second[:, tail] + picked_second[:, tail + 1]
    both = picked_first + picked_second
    stat_second = both[:, tail + 2] + both[:, tail + 3]
    grad_hidden_loc = both[:, part_width:tail]
    grad_local = cotangent.astype(F32)
    _, pull_gates = jax.vjp(lambda given: gate_pair(given, hot_first, hot_second), logits)
    (grad_logits,) = pull_gates((kept[:, 0] * share_first_grad, kept[:, 1] * share_second_grad))
    grad_logits_low = grad_logits.astype(BF)
    grad_router_rows = rows_rows(grad_logits_low, router_w)
    stat_total = stat_second + jnp.sum(normed_second * gain_second * grad_router_rows, 1)

    def take_cols(full_rows):
        return lax.dynamic_slice_in_dim(full_rows, narrow_at * part_width, part_width, 1)

    grad_hidden_loc = grad_hidden_loc + take_cols(grad_router_rows)
    normed_second_loc = take_cols(normed_second)
    grad_gain_second = jnp.sum(grad_hidden_loc * normed_second_loc, 0)
    grad_middle = grad_local + scale_second * (
        gain_second_loc * grad_hidden_loc - normed_second_loc * stat_total[:, None] / full_width
    )
    grad_router_w = cols_cols(hidden_second, grad_logits_low)
    grad_branch = lax.all_gather(grad_middle.astype(BF), "narrow", axis=1, tiled=True)
    grad_attended = rows_cols(grad_branch, out_w).astype(BF)
    grad_out_w = cols_cols(grad_branch, attended)
    grad_qs, grad_ks, grad_vs = [], [], []
    for head in range(heads):
        query, key, value, weights = saved[head]
        grad_out = head_cols(grad_attended, head)
        grad_weights = rows_rows(grad_out, value)
        inner = jnp.sum(weights * grad_weights, -1, keepdims=True)
        grad_scores = (weights * (grad_weights - inner)).astype(BF)
        grad_q = rows_cols(grad_scores, key) * score_scale
        grad_k = cols_cols(grad_scores, query) * score_scale
        grad_qs.append(rotate(grad_q, cosines, -sines).astype(BF))
        grad_ks.append(rotate(grad_k, cosines, -sines).astype(BF))
        grad_vs.append(cols_cols(weights.astype(BF), grad_out).astype(BF))
    grad_query_raw = jnp.concatenate(grad_qs, 1)
    grad_key_raw = jnp.concatenate(grad_ks, 1)
    grad_value_raw = jnp.concatenate(grad_vs, 1)
    grad_hidden_first = (
        rows_rows(grad_query_raw, query_w)
        + rows_rows(grad_key_raw, key_w)
        + rows_rows(grad_value_raw, value_w)
    )
    stat_first = jnp.sum(normed_first * gain_first * grad_hidden_first, 1, keepdims=True)
    extras = jnp.pad(jnp.concatenate(two_parts(stat_first), 1), ((0, 0), (0, 126)))
    grad_hidden_low = grad_hidden_first.astype(BF)
    first_parts = []
    for part in range(narrow_count):
        first_parts += [grad_hidden_low[:, part * part_width : (part + 1) * part_width], extras]
    first_back = lax.psum_scatter(
        jnp.concatenate(first_parts, 1), "narrow", scatter_dimension=1, tiled=True
    ).astype(F32)
    grad_first_loc = first_back[:, :part_width]
    stat_first = first_back[:, part_width : part_width + 1]
    stat_first = stat_first + first_back[:, part_width + 1 : part_width + 2]
    normed_first_loc = take_cols(normed_first)
    grad_gain_first = jnp.sum(grad_first_loc * normed_first_loc, 0)
    grad_tokens = grad_middle + scale_first * (
        gain_first_loc * grad_first_loc - normed_first_loc * stat_first / full_width
    )
    grad_attn_w = jnp.concatenate(
        [
            cols_cols(hidden_first, grad_query_raw).astype(BF),
            cols_cols(hidden_first, grad_key_raw).astype(BF),
            cols_cols(hidden_first, grad_value_raw).astype(BF),
            grad_out_w.astype(BF),
        ],
        1,
    )
    attn_summed = lax.psum_scatter(
        grad_attn_w, "wide", scatter_dimension=0, tiled=True
    ).astype(F32)
    router_summed = lax.psum_scatter(grad_router_w, "wide", scatter_dimension=0, tiled=True)
    gains_summed = lax.psum(jnp.stack([grad_gain_first, grad_gain_second]), "wide")
    return (
        output,
        grad_tokens,
        gains_summed[0],
        attn_summed[:, :part_width],
        attn_summed[:, part_width : 2 * part_width],
        attn_summed[:, 2 * part_width : 3 * part_width],
        attn_summed[:, 3 * part_width :],
        gains_summed[1],
        router_summed,
        gate_out,
        up_out,
        down_out,
    )


def per_device(
    tokens, gain_attn, w_query, w_key, w_value, w_out, gain_ffn, w_router,
    w_gate, w_up, w_down, segment, parents, expert_ids, slot_order, cotangent,
):
    if lax.axis_size("wide") != 8 or lax.axis_size("narrow") != 4:
        return plain_device(
            tokens, gain_attn, w_query, w_key, w_value, w_out, gain_ffn, w_router,
            w_gate, w_up, w_down, segment, parents, expert_ids, slot_order, cotangent,
        )
    (
        in_w, out_w, expert_w, slot_mid, slot_grad, slot_gate, middle, hidden_first,
        token_parts, qkv, probs, attended, stat, rope, picks, columns,
    ) = front_call(
        tokens, cotangent, jnp.stack([gain_attn, gain_ffn]), (w_query, w_key, w_value, w_out),
        w_router.T, (w_gate, w_up, w_down), segment, parents, expert_ids.T, slot_order,
    )
    back_mid, back_exp, last_exp, back_ext, grads, early_experts = mid_call(
        slot_mid, slot_grad, slot_gate, token_parts, expert_w
    )
    (
        output, grad_tokens, summed, small, router, experts,
    ) = tail_call(
        back_mid, back_exp, last_exp, back_ext, grads, picks, stat, columns, middle, cotangent, tokens,
        token_parts, qkv, probs, attended, rope, hidden_first, in_w, out_w,
    )
    gate_out, up_out, down_out, output, grad_tokens, grad_q, grad_k, grad_v, grad_o = finish_call(
        early_experts, experts, output, grad_tokens, summed
    )
    return (
        output, grad_tokens, small[5], grad_q, grad_k, grad_v, grad_o, small[4],
        router[:EXPERTS].T, gate_out, up_out, down_out,
    )


def solution(mesh):
    pair = P("wide", "narrow")
    part = P("narrow")
    rows = P("wide", None)
    cube = P("wide", None, "narrow")
    return jax.shard_map(
        per_device,
        mesh=mesh,
        in_specs=(
            pair, part, pair, pair, pair, pair, part, rows, cube, cube, cube,
            rows, rows, rows, rows, pair,
        ),
        out_specs=(
            pair, pair, part, pair, pair, pair, pair, part, rows, cube, cube, cube,
        ),
        check_vma=False,
    )
```

profile of v0, /device:TPU:0, one launch (start us, length us, event | category | flops | bytes accessed | tf_op | source)
XLA Modules:
  0.0 379.2 jit_solution(11553473957926339116)
XLA Ops:
  0.6 0.7 stack.9
  1.3 0.7 stack.10
  2.0 0.6 pad_maximum_fusion.gains_ref
  2.6 166.2 %front.1 = (bf16[8,256,1664]{2,1,0:T(8,128)(2,1)}, bf16[8,256,512]{2,1,0:T(8,128)(2,1)}, bf16[3,4,2,256,1408]{4,3,2,1,0:T(8,128)(2,1)}, bf16[576,2048]{1,0:T(8,1...) custom-call(bf16[256,512]{1,0:T(8,128)(2,1)} %tok_ref.3, ...), custom_call_target="tpu_custom_call" | custom-call | flops 6000000000 | bytes 60000000 | tf_op jit(solution)/shard_map/front/pallas_call | solution.py:682
  168.8 96.7 %mid.1 = (bf16[576,512]{1,0:T(8,128)(2,1)}, bf16[576,512]{1,0:T(8,128)(2,1)}, bf16[576,512]{1,0:T(8,128)(2,1)}, bf16[576,128]{1,0:T(8,128)(2,1)}, bf16[1024,1408...) custom-call(bf16[576,2048]{1,0:T(8,128)(2,1)} %get-tuple-element.49.x_ref, bf16[576,2048]{1,0:T(8,128)(2,1)} %get-tuple-element.50.dy_ref, ...), custom_call_target="tpu_custom_call" | custom-call | flops 30000001024 | bytes 40000000 | tf_op jit(solution)/shard_map/mid/pallas_call | solution.py:973
  265.6 97.4 %tail.1 = (bf16[256,512]{1,0:T(8,128)(2,1)}, f32[256,512]{1,0:T(8,128)}, f32[256,2048]{1,0:T(8,128)}, f32[8,512]{1,0:T(8,128)}, f32[8,256]{1,0:T(8,128)}, /*index=5*/bf16[4,256,1408]{2,1,0:T(8,128)(2,1)}) custom-call(bf16[576,512]{1,0:T(8,128)(2,1)} %get-tuple-element.55.mid_ref, bf16[576,512]{1,0:T(8,128)(2,1)} %get-tuple-element.56.exp_ref, ...), custom_call_target="tpu_custom_call" | custom-call | flops 6000000000 | bytes 60000000 | tf_op jit(solution)/shard_map/tail/pallas_call | solution.py:1358
  363.0 1.3 slice_bitcast_fusion
  364.3 1.4 fusion
  365.7 13.3 %finish.1 = (f32[256,4,1408]{2,1,0:T(4,128)}, f32[256,4,1408]{2,1,0:T(4,128)}, f32[256,4,1408]{2,1,0:T(4,128)}, bf16[256,512]{1,0:T(8,128)(2,1)}, f32[256,512]{1...) custom-call(bf16[2,4,256,1408]{3,2,1,0:T(8,128)(2,1)} %get-tuple-element.54.down, ...), custom_call_target="tpu_custom_call" | custom-call | tf_op jit(solution)/shard_map/finish/pallas_call | solution.py:1446
where the time goes:
time: 380 us; the launch traced here: 379 us
  Pallas kernels  374 us (98%)
  local copies, waits for them, and re-layouts  4.03 us (1%)
    pallas_call x1, Pallas kernels, front_call(): pl.pallas_call(front_body, out_shape=(arr((8, rows_each, 1664), BF), arr(...  166 us
    pallas_call x1, Pallas kernels, tail_call(): pl.pallas_call(tail_body, out_shape=(arr(own, BF), arr(own, F32), arr((ro...  97.4 us
    pallas_call x1, Pallas kernels, mid_call(): pl.pallas_call(mid_body, out_shape=(arr((slots, part_width), BF), arr((sl...  96.7 us
    pallas_call x1, Pallas kernels, finish_call(): pl.pallas_call(finish_body, grid=(rows_each // step,), out_shape=(arr((ro...  13.3 us

commit v1 on v0

--- a/solution.py
+++ b/solution.py
@@ -345,16 +345,17 @@
         links.land(self.blocks.at[2 * self.chip + 1 - self.core], self.mate, self.mate_slots[3])
 
 
-FRONT_SLOTS = 104
+FRONT_SLOTS = 112
 
 
 def front_body(
-    tok_ref, cot_ref, gains_ref, wq_ref, wk_ref, wv_ref, wo_ref, router_ref, gate_ref, up_ref,
+    tok_ref, cot_ref, gain_first_ref, gain_second_ref, wq_ref, wk_ref, wv_ref, wo_ref, router_ref, gate_ref, up_ref,
     down_ref, segment_ref, parents_ref, ids_ref, rank_ref,
-    qkvw_out, outw_out, expert_out, x_out, dy_out, gate_out, middle_out, hidden_out,
-    tokens_out, qkv_out, prob_out, att_out, stat_out, rope_out, pick_out, cols_out,
-    raw_proj, seen_at, raw, moved_ref, pack, tok_pack, qkvw, outw, cot_send, y_send, br_send, br_recv, stat_send, stat_recv,
-    gate_send, sent, landed, local,
+    qkvw_out, outw_out, expert_out, x_out, dy_out, gate_out, middle_out, hidden_hbm,
+    tokens_hbm, qkv_hbm, prob_hbm, att_out, stat_out, rope_out, pick_hbm, cols_out,
+    hidden_out, tokens_out, qkv_out, prob_out, pick_out,
+    raw_proj, seen_at, raw, moved_ref, pack, tok_pack, qkvw, outw, cot_send, y_send, br_send,
+    br_recv, stat_send, stat_recv, gate_send, sent, landed, local,
 ):
     n = lax.axis_index("narrow")
     w = lax.axis_index("wide")
@@ -387,7 +388,11 @@
         lax.fori_loop(0, rows_each // 32, some_rows, 0)
 
     tok_pack[0:token_count, :] = tok_ref[...]
-    tok_pack[token_count : token_count + 2, :] = gains_ref[...]
+    for index, gain_ref in enumerate((gain_first_ref, gain_second_ref)):
+        for row in range(part_width // 128):
+            tok_pack[
+                token_count + index : token_count + index + 1, row * 128 : (row + 1) * 128
+            ] = gain_ref[row : row + 1, :]
     tokens_out[n] = tok_pack[...]
     tok_chain = Chain(links, n, lambda m: tokens_out.at[m])
     tok_chain.start(0)
@@ -507,35 +512,42 @@
     in_gather.finish()
     saved_in = links.move(qkvw, qkvw_out)
 
-    expert_slots = [[links.slot() for _ in range(NEAR)] for _ in range(3)]
-    expert_mate = [[links.slot() for _ in range(4)] for _ in range(3)]
-    def set_out(kind_at):
+    pieces = ((0, 0, rows_each), (1, 0, rows_each)) + tuple(
+        (2, half * rows_each // 2, rows_each // 2) for half in range(2)
+    )
+    expert_slots = [[links.slot() for _ in range(NEAR)] for _ in pieces]
+    expert_mate = [[links.slot() for _ in range(4)] for _ in pieces]
+
+    def piece_of(array, index):
+        return array.at[pl.ds(pieces[index][1], pieces[index][2]), :]
+
+    def landing(index, owner, side):
+        return piece_of(expert_out.at[pieces[index][0], owner, side], index)
+
+    def set_out(index):
+        kind_at = pieces[index][0]
         for step in range(NEAR):
             links.send(
-                moved_ref.at[kind_at, plane[step]], expert_out.at[kind_at, chip, core],
-                at_plane(plane[step]), expert_slots[kind_at][step],
+                piece_of(moved_ref.at[kind_at, plane[step]], index), landing(index, chip, core),
+                at_plane(plane[step]), expert_slots[index][step],
             )
-        links.send(
-            moved_ref.at[kind_at, chip], expert_out.at[kind_at, chip, core], mate,
-            expert_mate[kind_at][3],
-        )
-        links.move(moved_ref.at[kind_at, chip], expert_out.at[kind_at, chip, core])
+        own = piece_of(moved_ref.at[kind_at, chip], index)
+        links.send(own, landing(index, chip, core), mate, expert_mate[index][3])
+        links.move(own, landing(index, chip, core))
 
     set_out(0)
     set_out(1)
 
-    def pass_on(kind_at):
+    def pass_on(index):
         for step in range(NEAR):
-            block = expert_out.at[kind_at, plane[step], core]
-            links.land(block, at_plane(plane[step]), expert_slots[kind_at][step])
-            links.send(block, block, mate, expert_mate[kind_at][step])
-
-    def all_there(kind_at):
+            block = landing(index, plane[step], core)
+            links.land(block, at_plane(plane[step]), expert_slots[index][step])
+            links.send(block, block, mate, expert_mate[index][step])
+
+    def all_there(index):
         for step in range(NEAR):
-            links.land(
-                expert_out.at[kind_at, plane[step], 1 - core], mate, expert_mate[kind_at][step]
-            )
-        links.land(expert_out.at[kind_at, chip, 1 - core], mate, expert_mate[kind_at][3])
+            links.land(landing(index, plane[step], 1 - core), mate, expert_mate[index][step])
+        links.land(landing(index, chip, 1 - core), mate, expert_mate[index][3])
 
     dy_chain.land(0)
     dy_chain.start(1)
@@ -572,6 +584,11 @@
         return value
 
     lax.fori_loop(0, part_width // HEAD_DIM, one_head, 0)
+    for source, target in (
+        (hidden_out, hidden_hbm), (tokens_out, tokens_hbm), (qkv_out, qkv_hbm),
+        (prob_out, prob_hbm), (pick_out, pick_hbm),
+    ):
+        links.move(source, target)
 
     dy_chain.land(1)
     dy_chain.start(2)
@@ -608,8 +625,9 @@
     x_chains[0].start(0)
 
     set_out(2)
-
-    gain_second = gains_ref[1:2, :].astype(F32)
+    set_out(3)
+
+    gain_second = tok_pack[token_count + 1 : token_count + 2, :].astype(F32)
     router = qkvw[pl.ds(2 * n, 2), :, 1536:1664].reshape(part_width, 128)
     logit_part = mm(router, (middle * gain_second).astype(BF), ((0,), (1,)))[0:8, :]
     square = middle * middle
@@ -663,12 +681,13 @@
     for step in range(NEAR):
         links.land(gate_rows(gate_out, plane[step]), at_plane(plane[step]), gate_slots[step])
     pass_on(2)
-    for kind_at in range(3):
-        all_there(kind_at)
+    pass_on(3)
+    for index in range(len(pieces)):
+        all_there(index)
     links.finish()
 
 
-def front_call(tokens, cotangent, gains, weights, router, experts, segment, parents, ids, rank):
+def front_call(tokens, cotangent, gain_attn, gain_ffn, weights, router, experts, segment, parents, ids, rank):
     token_count, part_width = tokens.shape
     full = 4 * part_width
     rows_each, _, hidden_width = experts[0].shape
@@ -699,9 +718,14 @@
             arr((2, SLOTS, token_count), BF),
             arr((token_count, 128), F32),
         ),
-        in_specs=[vmem] * 8 + [hbm] * 3 + [vmem] * 4,
-        out_specs=(hbm, hbm, hbm) + (vmem,) * 13,
+        in_specs=[vmem] * 9 + [hbm] * 3 + [vmem] * 4,
+        out_specs=(hbm,) * 5 + (vmem, vmem) + (hbm,) * 4 + (vmem,) * 3 + (hbm, vmem),
         scratch_shapes=[
+            pltpu.VMEM((token_count, full), BF),
+            pltpu.VMEM((4, token_count + 16, part_width), BF),
+            pltpu.VMEM((3, token_count, part_width), BF),
+            pltpu.VMEM((heads, token_count, token_count), F32),
+            pltpu.VMEM((2, SLOTS, token_count), BF),
             pltpu.VMEM((3, token_count, part_width), F32),
             pltpu.VMEM((token_count, token_count), F32),
             pltpu.VMEM((3, rows_each, EXPERTS, hidden_width), BF),
@@ -719,7 +743,7 @@
             pltpu.VMEM((SLOTS, 128), F32),
             pltpu.SemaphoreType.DMA((FRONT_SLOTS,)),
             pltpu.SemaphoreType.DMA((FRONT_SLOTS,)),
-            pltpu.SemaphoreType.DMA((16,)),
+            pltpu.SemaphoreType.DMA((24,)),
         ],
         compiler_params=pltpu.CompilerParams(
             collective_id=0, has_side_effects=True, vmem_limit_bytes=60 * 1024 * 1024
@@ -728,7 +752,10 @@
             flops=6_000_000_000, bytes_accessed=60_000_000, transcendentals=400_000
         ),
         name="front",
-    )(tokens, cotangent, gains, *weights, router, *experts, segment, parents, ids, rank)
+    )(
+        tokens, cotangent, gain_attn.reshape(-1, 128), gain_ffn.reshape(-1, 128), *weights,
+        router, *experts, segment, parents, ids, rank,
+    )
 
 
 MID_SLOTS = 48
@@ -738,9 +765,9 @@
 
 
 def mid_body(
-    x_ref, dy_ref, gate_ref, tokens_ref, w_ref,
+    x_ref, dy_hbm, gate_ref, tokens_ref, w_ref,
     back_mid_out, back_exp_out, last_exp_out, extra_out, grads_out, expert_out,
-    weights, hidden, graded_send, hidden_cat, graded_cat, act_cat, gate_cat, up_cat,
+    dy_ref, weights, hidden, graded_send, hidden_cat, graded_cat, act_cat, gate_cat, up_cat,
     turned, down_grad, rs_send, rs_recv, ext_send, ext_recv, sent, landed, local,
 ):
     n = lax.axis_index("narrow")
@@ -756,6 +783,7 @@
     half = full // 2
     hidden_width = weights.shape[2]
 
+    dy_load = links.move(dy_hbm, dy_ref)
     x_load = links.move(x_ref, hidden)
     loads = [
         links.move(
@@ -770,6 +798,7 @@
     greet(to_z, plane, chip, core, True)
 
     slot_gate = gate_ref[:, 0:1]
+    dy_load.wait()
     for c in range(4):
         theirs = pl.ds(pl.multiple_of((2 * c + 1 - core) * rows_each, rows_each), rows_each)
         ours = pl.ds(pl.multiple_of((2 * c + core) * rows_each, rows_each), rows_each)
@@ -980,9 +1009,10 @@
             arr((full // 2, hidden_width), BF),
             arr((2, 4, rows_each, hidden_width), BF),
         ),
-        in_specs=[hbm] + [vmem] * 3 + [hbm],
+        in_specs=[hbm] * 2 + [vmem] * 2 + [hbm],
         out_specs=(vmem,) * 4 + (hbm, hbm),
         scratch_shapes=[
+            pltpu.VMEM((slots, full), BF),
             pltpu.VMEM((3, full, hidden_width), BF),
             pltpu.VMEM((slots, full), BF),
             pltpu.VMEM((slots, full // 2), BF),
@@ -1049,11 +1079,12 @@
 
 
 def tail_body(
-    mid_ref, exp_ref, last_ref, ext_ref, moved_ref, picks_ref, stat_ref, cols_ref, middle_ref, cot_ref,
-    tok_ref, tokens_ref, qkv_ref, prob_ref, att_ref, rope_ref, hidden_ref, qkvw_ref, outw_ref,
+    mid_ref, exp_ref, last_ref, ext_ref, moved_ref, picks_hbm, stat_ref, cols_ref, middle_ref,
+    cot_ref, tok_ref, tokens_hbm, qkv_hbm, prob_hbm, att_ref, rope_ref, hidden_hbm, qkvw_ref,
+    outw_ref,
     output_out, grad_tokens_out, summed_out, small_out,
     router_out, expert_out,
-    grad_att_at, exp_in, exp_sum, router_all, qkvw, outw, ret_mid, ret_exp, ret_ext, branch, hidden_cat, branch_cat, att_cat, proj_cat,
+    picks_ref, tokens_ref, qkv_ref, prob_ref, hidden_ref, grad_att_at, exp_in, exp_sum, router_all, qkvw, outw, ret_mid, ret_exp, ret_ext, branch, hidden_cat, branch_cat, att_cat, proj_cat,
     proj_send, proj_recv, first_send, first_recv, col_send, col_recv, small_mate, small_sum,
     small_recv, last_mate, last_sum, last_recv, sent, landed, local,
 ):
@@ -1076,6 +1107,13 @@
     def cap_rows(array, owner):
         return array.at[pl.ds(pl.multiple_of(owner * CAP, 16), CAP), :]
 
+    first_loads = [
+        links.move(source, target)
+        for source, target in (
+            (hidden_hbm, hidden_ref), (picks_hbm, picks_ref), (tokens_hbm, tokens_ref),
+            (qkv_hbm, qkv_ref), (prob_hbm, prob_ref),
+        )
+    ]
     loads = [links.move(qkvw_ref, qkvw), links.move(outw_ref, outw)]
     links.waits = []
     greet(to_z, plane, chip, core, True)
@@ -1132,6 +1170,8 @@
             lands.append((target.at[1 - core, :, cols], slot))
         return lambda: [links.land(block, mate, slot) for block, slot in lands]
 
+    for load in first_loads:
+        load.wait()
     hidden_there = parity_exchange(hidden_ref, hidden_cat)
     att_cat[core] = att_ref[...]
     att_there = to_mate(att_ref, att_cat)
@@ -1365,9 +1405,14 @@
             arr((8, rows_each), F32),
             arr((4, rows_each, hidden_width), BF),
         ),
-        in_specs=[vmem] * 4 + [hbm] + [vmem] * 12 + [hbm] * 2,
+        in_specs=[vmem] * 4 + [hbm] * 2 + [vmem] * 5 + [hbm] * 3 + [vmem] * 2 + [hbm] * 3,
         out_specs=(vmem,) * 5 + (hbm,),
         scratch_shapes=[
+            pltpu.VMEM((2, slots, token_count), BF),
+            pltpu.VMEM((4, token_count + 16, part_width), BF),
+            pltpu.VMEM((3,) + own, BF),
+            pltpu.VMEM((part_width // HEAD_DIM, token_count, token_count), F32),
+            pltpu.VMEM((token_count, full), BF),
             pltpu.VMEM(own, BF),
             pltpu.VMEM((slots, part_width), BF),
             pltpu.VMEM((slots, part_width), BF),
@@ -1396,7 +1441,7 @@
             pltpu.VMEM((NEAR, 8, part_width), F32),
             pltpu.SemaphoreType.DMA((TAIL_SLOTS,)),
             pltpu.SemaphoreType.DMA((TAIL_SLOTS,)),
-            pltpu.SemaphoreType.DMA((16,)),
+            pltpu.SemaphoreType.DMA((24,)),
         ],
         compiler_params=pltpu.CompilerParams(
             collective_id=2, has_side_effects=True, vmem_limit_bytes=60 * 1024 * 1024
@@ -1409,8 +1454,9 @@
 
 
 def finish_body(
-    down_ref, gate_ref, up_ref, output_ref, tokens_ref, summed_ref,
-    gate_out, up_out, down_out, output_out, tokens_out, *proj_outs,
+    down_ref, gate_ref, up_ref, output_ref, tokens_ref, summed_ref, small_ref, router_ref,
+    gate_out, up_out, down_out, output_out, tokens_out, q_out, k_out, v_out, o_out,
+    gain_first_out, gain_second_out, router_out,
 ):
     def some_rows(index, value):
         rows = pl.ds(pl.multiple_of(index * 16, 16), 16)
@@ -1423,11 +1469,17 @@
     output_out[...] = output_ref[...]
     tokens_out[...] = tokens_ref[...]
     width = tokens_ref.shape[1]
-    for part, target in enumerate(proj_outs):
+    for part, target in enumerate((q_out, k_out, v_out, o_out)):
         target[...] = summed_ref[:, part * width : (part + 1) * width].astype(F32)
-
-
-def finish_call(early, late, output, grad_tokens, summed):
+    for row, target in ((5, gain_first_out), (4, gain_second_out)):
+        for index in range(width // 128):
+            target[index : index + 1, :] = small_ref[
+                row : row + 1, index * 128 : (index + 1) * 128
+            ]
+    router_out[...] = router_ref[0:EXPERTS, :]
+
+
+def finish_call(early, late, output, grad_tokens, summed, small, router):
     _, rows_each, hidden_width = late.shape
     token_count, part_width = output.shape
     step = 32
@@ -1437,6 +1489,9 @@
 
     def cube(which):
         return pl.BlockSpec((None, EXPERTS, step, hidden_width), lambda i: (which, 0, i, 0))
+
+    def same(shape):
+        return pl.BlockSpec(shape, lambda i: (0, 0))
 
     spread = pl.BlockSpec((step, EXPERTS, hidden_width), lambda i: (i, 0, 0))
 
@@ -1448,15 +1503,21 @@
         grid=(rows_each // step,),
         out_shape=(arr((rows_each, EXPERTS, hidden_width), F32),) * 3
         + (arr(output.shape, BF), arr(output.shape, F32))
-        + (arr((rows_each, part_width), F32),) * 4,
+        + (arr((rows_each, part_width), F32),) * 4
+        + (arr((part_width // 128, 128), F32),) * 2
+        + (arr((EXPERTS, rows_each), F32),),
         in_specs=[
             cube(0), cube(1),
             pl.BlockSpec((EXPERTS, step, hidden_width), lambda i: (0, i, 0)),
-            flat(part_width), flat(part_width), flat(4 * part_width),
+            flat(part_width), flat(part_width), flat(4 * part_width), same(small.shape),
+            same(router.shape),
         ],
-        out_specs=(spread,) * 3 + (flat(part_width),) * 6,
+        out_specs=(spread,) * 3
+        + (flat(part_width),) * 6
+        + (same((part_width // 128, 128)),) * 2
+        + (same((EXPERTS, rows_each)),),
         name="finish",
-    )(early, early, late, output, grad_tokens, summed)
+    )(early, early, late, output, grad_tokens, summed, small, router)
 
 
 def plain_device(
@@ -1724,7 +1785,7 @@
         in_w, out_w, expert_w, slot_mid, slot_grad, slot_gate, middle, hidden_first,
         token_parts, qkv, probs, attended, stat, rope, picks, columns,
     ) = front_call(
-        tokens, cotangent, jnp.stack([gain_attn, gain_ffn]), (w_query, w_key, w_value, w_out),
+        tokens, cotangent, gain_attn, gain_ffn, (w_query, w_key, w_value, w_out),
         w_router.T, (w_gate, w_up, w_down), segment, parents, expert_ids.T, slot_order,
     )
     back_mid, back_exp, last_exp, back_ext, grads, early_experts = mid_call(
@@ -1736,12 +1797,13 @@
         back_mid, back_exp, last_exp, back_ext, grads, picks, stat, columns, middle, cotangent, tokens,
         token_parts, qkv, probs, attended, rope, hidden_first, in_w, out_w,
     )
-    gate_out, up_out, down_out, output, grad_tokens, grad_q, grad_k, grad_v, grad_o = finish_call(
-        early_experts, experts, output, grad_tokens, summed
-    )
+    (
+        gate_out, up_out, down_out, output, grad_tokens, grad_q, grad_k, grad_v, grad_o,
+        grad_gain_first, grad_gain_second, router,
+    ) = finish_call(early_experts, experts, output, grad_tokens, summed, small, router)
     return (
-        output, grad_tokens, small[5], grad_q, grad_k, grad_v, grad_o, small[4],
-        router[:EXPERTS].T, gate_out, up_out, down_out,
+        output, grad_tokens, grad_gain_first.reshape(-1), grad_q, grad_k, grad_v, grad_o,
+        grad_gain_second.reshape(-1), router.T, gate_out, up_out, down_out,
     )
 
 

time: 380 us -> 371 us (0.976)
  local copies, waits for them, and re-layouts: 4.03 us -> 0 us
  Pallas kernels: 374 us -> 370 us
where the time goes in v1:
time: 371 us
  Pallas kernels  370 us (100%)
    pallas_call x1, Pallas kernels, front_call(): pl.pallas_call(front_body, out_shape=(arr((8, rows_each, 1664), BF), arr(...  164 us
    pallas_call x1, Pallas kernels, mid_call(): pl.pallas_call(mid_body, out_shape=(arr((slots, part_width), BF), arr((sl...  96.7 us
    pallas_call x1, Pallas kernels, tail_call(): pl.pallas_call(tail_body, out_shape=(arr(own, BF), arr(own, F32), arr((ro...  95.8 us
    pallas_call x1, Pallas kernels, finish_call(): pl.pallas_call(finish_body, grid=(rows_each // step,), out_shape=(arr((ro...  13.5 us

profile of v1, /device:TPU:0, one launch (start us, length us, event | category | flops | bytes accessed | tf_op | source)
XLA Modules:
  0.0 370.7 jit_solution(11537535148718389449)
XLA Ops:
  0.6 163.9 %front.1 = (bf16[8,256,1664]{2,1,0:T(8,128)(2,1)}, bf16[8,256,512]{2,1,0:T(8,128)(2,1)}, bf16[3,4,2,256,1408]{4,3,2,1,0:T(8,128)(2,1)}, bf16[576,2048]{1,0:T(8,1...) custom-call(bf16[256,512]{1,0:T(8,128)(2,1)} %tok_ref.3, ...), custom_call_target="tpu_custom_call" | custom-call | flops 6000000000 | bytes 60000000 | tf_op jit(solution)/shard_map/front/pallas_call | solution.py:701
  164.6 96.7 %mid.1 = (bf16[576,512]{1,0:T(8,128)(2,1)}, bf16[576,512]{1,0:T(8,128)(2,1)}, bf16[576,512]{1,0:T(8,128)(2,1)}, bf16[576,128]{1,0:T(8,128)(2,1)}, bf16[1024,1408...) custom-call(bf16[576,2048]{1,0:T(8,128)(2,1)} %get-tuple-element.52.x_ref, bf16[576,2048]{1,0:T(8,128)(2,1)} %get-tuple-element.53.dy_hbm, ...), custom_call_target="tpu_custom_call" | custom-call | flops 30000001024 | bytes 40000000 | tf_op jit(solution)/shard_map/mid/pallas_call | solution.py:1002
  261.2 95.8 %tail.1 = (bf16[256,512]{1,0:T(8,128)(2,1)}, f32[256,512]{1,0:T(8,128)}, f32[256,2048]{1,0:T(8,128)}, f32[8,512]{1,0:T(8,128)}, f32[8,256]{1,0:T(8,128)}, /*index=5*/bf16[4,256,1408]{2,1,0:T(8,128)(2,1)}) custom-call(bf16[576,512]{1,0:T(8,128)(2,1)} %get-tuple-element.58.mid_ref, bf16[576,512]{1,0:T(8,128)(2,1)} %get-tuple-element.59.exp_ref, ...), custom_call_target="tpu_custom_call" | custom-call | flops 6000000000 | bytes 60000000 | tf_op jit(solution)/shard_map/tail/pallas_call | solution.py:1398
  357.1 13.5 %finish.1 = (f32[256,4,1408]{2,1,0:T(4,128)}, f32[256,4,1408]{2,1,0:T(4,128)}, f32[256,4,1408]{2,1,0:T(4,128)}, bf16[256,512]{1,0:T(8,128)(2,1)}, f32[256,512]{1...) custom-call(bf16[2,4,256,1408]{3,2,1,0:T(8,128)(2,1)} %get-tuple-ele, ...), custom_call_target="tpu_custom_call" | custom-call | tf_op jit(solution)/shard_map/finish/pallas_call | solution.py:1501

commit v2 on v1

--- a/solution.py
+++ b/solution.py
@@ -1453,71 +1453,95 @@
     )(*args)
 
 
+FINISH_ROWS = 64
+
+
 def finish_body(
-    down_ref, gate_ref, up_ref, output_ref, tokens_ref, summed_ref, small_ref, router_ref,
+    early_ref, late_ref, output_ref, tokens_ref, summed_ref, small_ref, router_ref,
     gate_out, up_out, down_out, output_out, tokens_out, q_out, k_out, v_out, o_out,
     gain_first_out, gain_second_out, router_out,
+    packed, spread, incoming, outgoing, passing,
 ):
-    def some_rows(index, value):
-        rows = pl.ds(pl.multiple_of(index * 16, 16), 16)
-        for source, target in ((gate_ref, gate_out), (up_ref, up_out), (down_ref, down_out)):
+    rows_each = packed.shape[2]
+    width = tokens_ref.shape[1]
+    sources = (early_ref.at[0], early_ref.at[1], late_ref)
+    targets = (down_out, gate_out, up_out)
+    loads = {}
+    for kind in range(3):
+        for part in range(rows_each // FINISH_ROWS):
+            rows = pl.ds(part * FINISH_ROWS, FINISH_ROWS)
+            loads[kind, part] = pltpu.make_async_copy(
+                sources[kind].at[:, rows, :], packed.at[kind, :, rows, :], incoming.at[kind, part]
+            )
+            loads[kind, part].start()
+    whole = [(output_ref, output_out), (tokens_ref, tokens_out)]
+    for part, target in enumerate((q_out, k_out, v_out, o_out)):
+        whole.append((summed_ref.at[:, pl.ds(part * width, width)], target))
+    copies = [
+        pltpu.make_async_copy(source, target, passing.at[index])
+        for index, (source, target) in enumerate(whole)
+    ]
+    stores = []
+    for (kind, part), load in loads.items():
+        load.wait()
+
+        def some_rows(index, value):
+            first = pl.multiple_of(part * FINISH_ROWS + index * 16, 16)
+            rows = pl.ds(first, 16)
             for expert in range(EXPERTS):
-                target[rows, expert, :] = source[expert, rows, :].astype(F32)
-        return value
-
-    lax.fori_loop(0, tokens_ref.shape[0] // 16, some_rows, 0)
-    output_out[...] = output_ref[...]
-    tokens_out[...] = tokens_ref[...]
-    width = tokens_ref.shape[1]
-    for part, target in enumerate((q_out, k_out, v_out, o_out)):
-        target[...] = summed_ref[:, part * width : (part + 1) * width].astype(F32)
+                spread[kind, rows, expert, :] = packed[kind, expert, rows, :].astype(F32)
+            return value
+
+        lax.fori_loop(0, FINISH_ROWS // 16, some_rows, 0)
+        rows = pl.ds(part * FINISH_ROWS, FINISH_ROWS)
+        stores.append(
+            pltpu.make_async_copy(
+                spread.at[kind, rows], targets[kind].at[rows], outgoing.at[kind, part]
+            )
+        )
+        stores[-1].start()
+        if kind == 0 and part == 0:
+            for copy in copies:
+                copy.start()
     for row, target in ((5, gain_first_out), (4, gain_second_out)):
         for index in range(width // 128):
             target[index : index + 1, :] = small_ref[
                 row : row + 1, index * 128 : (index + 1) * 128
             ]
     router_out[...] = router_ref[0:EXPERTS, :]
+    for copy in stores + copies:
+        copy.wait()
 
 
 def finish_call(early, late, output, grad_tokens, summed, small, router):
     _, rows_each, hidden_width = late.shape
-    token_count, part_width = output.shape
-    step = 32
-
-    def flat(width):
-        return pl.BlockSpec((step, width), lambda i: (i, 0))
-
-    def cube(which):
-        return pl.BlockSpec((None, EXPERTS, step, hidden_width), lambda i: (which, 0, i, 0))
-
-    def same(shape):
-        return pl.BlockSpec(shape, lambda i: (0, 0))
-
-    spread = pl.BlockSpec((step, EXPERTS, hidden_width), lambda i: (i, 0, 0))
+    part_width = output.shape[1]
+    vmem = pl.BlockSpec(memory_space=pltpu.VMEM)
+    hbm = pl.BlockSpec(memory_space=pl.ANY)
+    parts = rows_each // FINISH_ROWS
 
     def arr(shape, dtype):
         return jax.ShapeDtypeStruct(shape, dtype)
 
     return pl.pallas_call(
         finish_body,
-        grid=(rows_each // step,),
         out_shape=(arr((rows_each, EXPERTS, hidden_width), F32),) * 3
         + (arr(output.shape, BF), arr(output.shape, F32))
         + (arr((rows_each, part_width), F32),) * 4
         + (arr((part_width // 128, 128), F32),) * 2
         + (arr((EXPERTS, rows_each), F32),),
-        in_specs=[
-            cube(0), cube(1),
-            pl.BlockSpec((EXPERTS, step, hidden_width), lambda i: (0, i, 0)),
-            flat(part_width), flat(part_width), flat(4 * part_width), same(small.shape),
-            same(router.shape),
+        in_specs=[hbm] * 2 + [vmem] * 5,
+        out_specs=(hbm,) * 9 + (vmem,) * 3,
+        scratch_shapes=[
+            pltpu.VMEM((3, EXPERTS, rows_each, hidden_width), BF),
+            pltpu.VMEM((3, rows_each, EXPERTS, hidden_width), F32),
+            pltpu.SemaphoreType.DMA((3, parts)),
+            pltpu.SemaphoreType.DMA((3, parts)),
+            pltpu.SemaphoreType.DMA((6,)),
         ],
-        out_specs=(spread,) * 3
-        + (flat(part_width),) * 6
-        + (same((part_width // 128, 128)),) * 2
-        + (same((EXPERTS, rows_each)),),
+        compiler_params=pltpu.CompilerParams(vmem_limit_bytes=56 * 1024 * 1024),
         name="finish",
-    )(early, early, late, output, grad_tokens, summed, small, router)
+    )(early, late, output, grad_tokens, summed, small, router)
 
 
 def plain_device(

time: 371 us -> 374 us (level); the launches traced: 371 us -> 369 us
  no operation moved by 1% of the time
where the time goes in v2:
time: 374 us; the launch traced here: 369 us
  Pallas kernels  368 us (98%)
    pallas_call x1, Pallas kernels, front_call(): pl.pallas_call(front_body, out_shape=(arr((8, rows_each, 1664), BF), arr(...  164 us
    pallas_call x1, Pallas kernels, mid_call(): pl.pallas_call(mid_body, out_shape=(arr((slots, part_width), BF), arr((sl...  96.7 us
    pallas_call x1, Pallas kernels, tail_call(): pl.pallas_call(tail_body, out_shape=(arr(own, BF), arr(own, F32), arr((ro...  95.8 us
    pallas_call x1, Pallas kernels, finish_call(): pl.pallas_call(finish_body, out_shape=(arr((rows_each, EXPERTS, hidden_wi...  11.7 us

profile of v2, /device:TPU:0, one launch (start us, length us, event | category | flops | bytes accessed | tf_op | source)
XLA Modules:
  0.0 369.2 jit_solution(8380602769646928942)
XLA Ops:
  0.6 163.9 %front.1 = (bf16[8,256,1664]{2,1,0:T(8,128)(2,1)}, bf16[8,256,512]{2,1,0:T(8,128)(2,1)}, bf16[3,4,2,256,1408]{4,3,2,1,0:T(8,128)(2,1)}, bf16[576,2048]{1,0:T(8,1...) custom-call(bf16[256,512]{1,0:T(8,128)(2,1)} %tok_ref.3, ...), custom_call_target="tpu_custom_call" | custom-call | flops 6000000000 | bytes 60000000 | tf_op jit(solution)/shard_map/front/pallas_call | solution.py:701
  164.6 96.7 %mid.1 = (bf16[576,512]{1,0:T(8,128)(2,1)}, bf16[576,512]{1,0:T(8,128)(2,1)}, bf16[576,512]{1,0:T(8,128)(2,1)}, bf16[576,128]{1,0:T(8,128)(2,1)}, bf16[1024,1408...) custom-call(bf16[576,2048]{1,0:T(8,128)(2,1)} %get-tuple-element.52.x_ref, bf16[576,2048]{1,0:T(8,128)(2,1)} %get-tuple-element.53.dy_hbm, ...), custom_call_target="tpu_custom_call" | custom-call | flops 30000001024 | bytes 40000000 | tf_op jit(solution)/shard_map/mid/pallas_call | solution.py:1002
  261.2 95.8 %tail.1 = (bf16[256,512]{1,0:T(8,128)(2,1)}, f32[256,512]{1,0:T(8,128)}, f32[256,2048]{1,0:T(8,128)}, f32[8,512]{1,0:T(8,128)}, f32[8,256]{1,0:T(8,128)}, /*index=5*/bf16[4,256,1408]{2,1,0:T(8,128)(2,1)}) custom-call(bf16[576,512]{1,0:T(8,128)(2,1)} %get-tuple-element.58.mid_ref, bf16[576,512]{1,0:T(8,128)(2,1)} %get-tuple-element.59.exp_ref, ...), custom_call_target="tpu_custom_call" | custom-call | flops 6000000000 | bytes 60000000 | tf_op jit(solution)/shard_map/tail/pallas_call | solution.py:1398
  357.1 11.7 %finish.1 = (f32[256,4,1408]{2,1,0:T(4,128)}, f32[256,4,1408]{2,1,0:T(4,128)}, f32[256,4,1408]{2,1,0:T(4,128)}, bf16[256,512]{1,0:T(8,128)(2,1)}, f32[256,512]{1...) custom-call(bf16[2,4,256,1408]{3,2,1,0:T(8,128)(2,1)} %get-tuple-ele, ...), custom_call_target="tpu_custom_call" | custom-call | tf_op jit(solution)/shard_map/finish/pallas_call | solution.py:1526

commit v3 on v2

--- a/solution.py
+++ b/solution.py
@@ -1453,7 +1453,7 @@
     )(*args)
 
 
-FINISH_ROWS = 64
+FINISH_ROWS = 128
 
 
 def finish_body(

time: 374 us -> 369 us (0.987); the launches traced: 369 us -> 369 us
  no operation moved by 1% of the time
where the time goes in v3:
time: 369 us
  Pallas kernels  368 us (100%)
    pallas_call x1, Pallas kernels, front_call(): pl.pallas_call(front_body, out_shape=(arr((8, rows_each, 1664), BF), arr(...  164 us
    pallas_call x1, Pallas kernels, mid_call(): pl.pallas_call(mid_body, out_shape=(arr((slots, part_width), BF), arr((sl...  96.7 us
    pallas_call x1, Pallas kernels, tail_call(): pl.pallas_call(tail_body, out_shape=(arr(own, BF), arr(own, F32), arr((ro...  95.8 us
    pallas_call x1, Pallas kernels, finish_call(): pl.pallas_call(finish_body, out_shape=(arr((rows_each, EXPERTS, hidden_wi...  11.5 us

profile of v3, /device:TPU:0, one launch (start us, length us, event | category | flops | bytes accessed | tf_op | source)
XLA Modules:
  0.0 368.7 jit_solution(10721780145757279819)
XLA Ops:
  0.6 163.9 %front.1 = (bf16[8,256,1664]{2,1,0:T(8,128)(2,1)}, bf16[8,256,512]{2,1,0:T(8,128)(2,1)}, bf16[3,4,2,256,1408]{4,3,2,1,0:T(8,128)(2,1)}, bf16[576,2048]{1,0:T(8,1...) custom-call(bf16[256,512]{1,0:T(8,128)(2,1)} %tok_ref.3, ...), custom_call_target="tpu_custom_call" | custom-call | flops 6000000000 | bytes 60000000 | tf_op jit(solution)/shard_map/front/pallas_call | solution.py:701
  164.6 96.7 %mid.1 = (bf16[576,512]{1,0:T(8,128)(2,1)}, bf16[576,512]{1,0:T(8,128)(2,1)}, bf16[576,512]{1,0:T(8,128)(2,1)}, bf16[576,128]{1,0:T(8,128)(2,1)}, bf16[1024,1408...) custom-call(bf16[576,2048]{1,0:T(8,128)(2,1)} %get-tuple-element.52.x_ref, bf16[576,2048]{1,0:T(8,128)(2,1)} %get-tuple-element.53.dy_hbm, ...), custom_call_target="tpu_custom_call" | custom-call | flops 30000001024 | bytes 40000000 | tf_op jit(solution)/shard_map/mid/pallas_call | solution.py:1002
  261.2 95.8 %tail.1 = (bf16[256,512]{1,0:T(8,128)(2,1)}, f32[256,512]{1,0:T(8,128)}, f32[256,2048]{1,0:T(8,128)}, f32[8,512]{1,0:T(8,128)}, f32[8,256]{1,0:T(8,128)}, /*index=5*/bf16[4,256,1408]{2,1,0:T(8,128)(2,1)}) custom-call(bf16[576,512]{1,0:T(8,128)(2,1)} %get-tuple-element.58.mid_ref, bf16[576,512]{1,0:T(8,128)(2,1)} %get-tuple-element.59.exp_ref, ...), custom_call_target="tpu_custom_call" | custom-call | flops 6000000000 | bytes 60000000 | tf_op jit(solution)/shard_map/tail/pallas_call | solution.py:1398
  357.1 11.5 %finish.1 = (f32[256,4,1408]{2,1,0:T(4,128)}, f32[256,4,1408]{2,1,0:T(4,128)}, f32[256,4,1408]{2,1,0:T(4,128)}, bf16[256,512]{1,0:T(8,128)(2,1)}, f32[256,512]{1...) custom-call(bf16[2,4,256,1408]{3,2,1,0:T(8,128)(2,1)} %get-tuple-ele, ...), custom_call_target="tpu_custom_call" | custom-call | tf_op jit(solution)/shard_map/finish/pallas_call | solution.py:1526

commit v4 on v3

--- a/solution.py
+++ b/solution.py
@@ -907,8 +907,8 @@
         links.move(block(chip), expert_out.at[index, chip])
 
     graded_there()
+    turned[...] = graded_cat[...].reshape(2 * slots, half).T
     acts_there[0]()
-    turned[...] = graded_cat[...].reshape(2 * slots, half).T
     weight_grad(act_cat, down_grad)
     share_out(0, down_grad)
 

time: 369 us -> 368 us (level)
  no operation moved by 1% of the time
where the time goes in v4:
time: 368 us
  Pallas kernels  367 us (100%)
    pallas_call x1, Pallas kernels, front_call(): pl.pallas_call(front_body, out_shape=(arr((8, rows_each, 1664), BF), arr(...  164 us
    pallas_call x1, Pallas kernels, mid_call(): pl.pallas_call(mid_body, out_shape=(arr((slots, part_width), BF), arr((sl...  96 us
    pallas_call x1, Pallas kernels, tail_call(): pl.pallas_call(tail_body, out_shape=(arr(own, BF), arr(own, F32), arr((ro...  95.8 us
    pallas_call x1, Pallas kernels, finish_call(): pl.pallas_call(finish_body, out_shape=(arr((rows_each, EXPERTS, hidden_wi...  11.5 us

profile of v4, /device:TPU:0, one launch (start us, length us, event | category | flops | bytes accessed | tf_op | source)
XLA Modules:
  0.0 368.1 jit_solution(11457699258024338387)
XLA Ops:
  0.6 163.9 %front.1 = (bf16[8,256,1664]{2,1,0:T(8,128)(2,1)}, bf16[8,256,512]{2,1,0:T(8,128)(2,1)}, bf16[3,4,2,256,1408]{4,3,2,1,0:T(8,128)(2,1)}, bf16[576,2048]{1,0:T(8,1...) custom-call(bf16[256,512]{1,0:T(8,128)(2,1)} %tok_ref.3, ...), custom_call_target="tpu_custom_call" | custom-call | flops 6000000000 | bytes 60000000 | tf_op jit(solution)/shard_map/front/pallas_call | solution.py:701
  164.6 96.0 %mid.1 = (bf16[576,512]{1,0:T(8,128)(2,1)}, bf16[576,512]{1,0:T(8,128)(2,1)}, bf16[576,512]{1,0:T(8,128)(2,1)}, bf16[576,128]{1,0:T(8,128)(2,1)}, bf16[1024,1408...) custom-call(bf16[576,2048]{1,0:T(8,128)(2,1)} %get-tuple-element.52.x_ref, bf16[576,2048]{1,0:T(8,128)(2,1)} %get-tuple-element.53.dy_hbm, ...), custom_call_target="tpu_custom_call" | custom-call | flops 30000001024 | bytes 40000000 | tf_op jit(solution)/shard_map/mid/pallas_call | solution.py:1002
  260.6 95.8 %tail.1 = (bf16[256,512]{1,0:T(8,128)(2,1)}, f32[256,512]{1,0:T(8,128)}, f32[256,2048]{1,0:T(8,128)}, f32[8,512]{1,0:T(8,128)}, f32[8,256]{1,0:T(8,128)}, /*index=5*/bf16[4,256,1408]{2,1,0:T(8,128)(2,1)}) custom-call(bf16[576,512]{1,0:T(8,128)(2,1)} %get-tuple-element.58.mid_ref, bf16[576,512]{1,0:T(8,128)(2,1)} %get-tuple-element.59.exp_ref, ...), custom_call_target="tpu_custom_call" | custom-call | flops 6000000000 | bytes 60000000 | tf_op jit(solution)/shard_map/tail/pallas_call | solution.py:1398
  356.4 11.5 %finish.1 = (f32[256,4,1408]{2,1,0:T(4,128)}, f32[256,4,1408]{2,1,0:T(4,128)}, f32[256,4,1408]{2,1,0:T(4,128)}, bf16[256,512]{1,0:T(8,128)(2,1)}, f32[256,512]{1...) custom-call(bf16[2,4,256,1408]{3,2,1,0:T(8,128)(2,1)} %get-tuple-ele, ...), custom_call_target="tpu_custom_call" | custom-call | tf_op jit(solution)/shard_map/finish/pallas_call | solution.py:1526
